TPU v7x, 512 devices: a whole 4x8x8 slice. The times are simulated.
512 devices in a mesh: layer: 4 (over x), expert: 128 (over z, y, core).
Axes of the slice: x: 4, y: 8, z: 8, core: 2. Of those that a mesh axis runs over, the one named last changes fastest.
Arguments:
- rows: bfloat16 [65536, 2048], P(('layer', 'expert')), parts along dimension 0, may hold values from -6 to 6
- expert_ids: int32 [65536, 8], P(('layer', 'expert')), parts along dimension 0, may hold values from 0 to 127, all different within a row; in each aligned block of 128 rows (0 to 127, 128 to 255, ...) at most 10 rows name the same one
- start_basis: float32 [8192, 128], P(('layer', 'expert')), parts along dimension 0, may hold values from -6 to 6
- weights: bfloat16 [512, 768, 2048], P(('layer', 'expert')), parts along dimension 0, may hold values from -0.125 to 0.125
Outputs:
- compressed: bfloat16 [512, 768, 128], P(('layer', 'expert')), parts along dimension 0
- basis: float32 [8192, 128], P(('layer', 'expert')), parts along dimension 0
There are 4 independent parts, one for each index of `layer`. A program takes and returns all parts, laid end to end along the dimension named above; each array names one. Nothing has to cross between parts.
Inputs may be any that keep to these rules, and one draw needn't show every extreme that they name: `expert_ids`: each row names 8 different experts; among the 128 rows of one device no expert is named by more than 10 rows, a bound that some blocks reach.
All inputs are finite; a program needn't handle non-finite values.
Results may differ from a plain program's by a relative error of at most 0.0075.
Values may be sent and summed in bfloat16 or wider, within the bound.
No kernel may reach another device: no remote copies, remote signals or barrier semaphores. Data moves between devices by JAX's collectives and lax.ppermute only.
A program may use at most 64 MiB of HBM per device.

v0:
```python
import jax
import jax.numpy as jnp
from jax import lax
from jax.sharding import PartitionSpec as P

NS_STEPS = 3


epsilon = 1e-06
coef_a = 3.4445
coef_b = -4.775
coef_c = 2.0315


def slot_table(block_ids, experts, capacity, row_count, top_count):
    flat_ids = block_ids.reshape(-1)
    onehot = (flat_ids[:, None] == jnp.arange(experts, dtype=jnp.int32)[None, :]).astype(jnp.int32)
    before = jnp.cumsum(onehot, axis=0) - onehot
    slot_rank = jnp.sum(before * onehot, axis=1)
    position = flat_ids * capacity + slot_rank
    source_row = jnp.arange(flat_ids.shape[0], dtype=jnp.int32) // top_count
    empty = jnp.full((experts * capacity,), row_count, jnp.int32)
    return empty.at[position].set(source_row)


def basis_term(received, weights, basis_bf):
    first = jnp.einsum(
        "esd,dr->esr", received, basis_bf, preferred_element_type=jnp.float32
    ).astype(jnp.bfloat16)
    second = jnp.einsum("esd,esr->edr", received, first, preferred_element_type=jnp.float32).astype(
        jnp.bfloat16
    )
    inner = jnp.einsum("efd,edr->efr", weights, second, preferred_element_type=jnp.float32).astype(
        jnp.bfloat16
    )
    back = jnp.einsum("efd,efr->edr", weights, inner, preferred_element_type=jnp.float32).astype(
        jnp.bfloat16
    )
    again = jnp.einsum("esd,edr->esr", received, back, preferred_element_type=jnp.float32).astype(
        jnp.bfloat16
    )
    return jnp.einsum("esd,esr->dr", received, again, preferred_element_type=jnp.float32)


def schulz_update(current, gram):
    square = jnp.dot(gram, gram, precision=lax.Precision.HIGHEST)
    return coef_a * current + jnp.dot(
        current, coef_b * gram + coef_c * square, precision=lax.Precision.HIGHEST
    )


def share_gram(current):
    local_gram = jnp.dot(current.T, current, precision=lax.Precision.HIGHEST)
    return lax.psum(local_gram, "expert")


def ortho_rows(term):
    shard = lax.psum_scatter(term, "expert", scatter_dimension=0, tiled=True)
    power = lax.psum(jnp.sum(shard * shard), "expert") + epsilon
    current = shard / jnp.sqrt(power)
    for inner_step in range(NS_STEPS):
        gram = share_gram(current)
        current = schulz_update(current, gram)
    return current


def shards(rows, expert_ids, start_basis, weights):
    row_count = rows.shape[0]
    top_count = expert_ids.shape[1]
    width = rows.shape[1]
    experts = lax.axis_size("expert") * weights.shape[0]
    capacity = max(2, min(row_count, row_count * top_count * 5 // (4 * experts)))
    values = rows.astype(jnp.float32)
    power = jnp.mean(values * values, axis=1, keepdims=True) + epsilon
    normed = (values / jnp.sqrt(power)).astype(jnp.bfloat16)
    padded = jnp.concatenate([normed, jnp.zeros((1, width), jnp.bfloat16)], axis=0)
    source_row = slot_table(expert_ids, experts, capacity, row_count, top_count)
    outgoing = padded[source_row].reshape(experts, capacity, width)
    received = lax.all_to_all(outgoing, "expert", split_axis=0, concat_axis=1, tiled=True)
    basis_bf = lax.all_gather(start_basis.astype(jnp.bfloat16), "expert", axis=0, tiled=True)
    term = basis_term(received, weights, basis_bf)
    local = ortho_rows(term)
    final_bf = lax.all_gather(local.astype(jnp.bfloat16), "expert", axis=0, tiled=True)
    compressed = jnp.einsum(
        "efd,dr->efr", weights, final_bf, preferred_element_type=jnp.float32
    ).astype(jnp.bfloat16)
    return (compressed, local)


def solution(mesh):
    in_specs = (
        P(("layer", "expert"), None),
        P(("layer", "expert"), None),
        P(("layer", "expert"), None),
        P(("layer", "expert"), None, None),
    )
    out_specs = (P(("layer", "expert"), None, None), P(("layer", "expert"), None))
    return jax.shard_map(shards, mesh=mesh, in_specs=in_specs, out_specs=out_specs, check_vma=False)
```

profile of v0, /device:TPU:1, one launch (start us, length us, event | category | flops | bytes accessed | tf_op | source)
XLA Modules:
  0.0 1436.8 jit_solution(6358131643358811545)
XLA Ops:
  7.2 0.9 copy.8
  8.1 0.1 eq.29
  8.2 0.1 eq.25
  8.3 0.7 broadcast_multiply_fusion
  9.0 0.1 copy.10
  9.1 0.2 fusion.28
  9.3 0.8 copy-done.1
  10.1 1.1 broadcast_add_fusion
  11.2 0.9 copy.11
  12.1 0.1 copy.7
  12.2 0.1 mul.55
  12.3 1.4 fusion.27
  13.7 4.3 scatter_custom_fusion
  18.1 1.2 fusion.23
  19.3 1.2 fusion.24
  20.5 0.9 concatenate.3
  21.4 11.9 gather_fusion
  33.4 9.5 reshape.102
  42.9 19.0 %all-to-all-start = ((bf16[128,10,2048]{2,1,0:T(8,128)(2,1)}), bf16[128,10,2048]{2,1,0:T(8,128)(2,1)}, u32[]{:S(2)}, u32[]{:S(2)}) async-start(bf16[128,10,2048]{2,1,0:T(8,128)(2,1)} %reshape.102), calls=%async_computation | async-start | bytes 16777216 | tf_op jit(solution)/shard_map/all_to_all | solution.py:79
  61.9 0.0 reduce-scatter.2.cloned.1.call-start
  62.0 293.3 %all_gather.6 = bf16[2048,128]{1,0:T(8,128)(2,1)} all-gather(bf16[16,128]{1,0:T(8,128)(2,1)S(1)} %convert_element_type.54), channel_id=1, replica_groups=mesh['layer'=4,'expert'=128] {'expert'}, dimensions={0}, use_global_device_ids=true | all-gather | bytes 528384 | tf_op jit(solution)/shard_map/all_gather | solution.py:80
  355.2 10.0 reshape.103
  365.3 10.3 convolution_convert_fusion
  375.6 3.9 fusion.6
  379.5 10.5 fusion.25
  390.0 0.0 all-reduce.5.cloned.1.call-start
  390.1 193.5 %reduce-scatter.2.cloned.1.call-done = f32[16,128]{1,0:T(8,128)} async-done(((f32[2048,128]{1,0:T(8,128)}), f32[16,128]{1,0:T(8,128)}) %reduce-scatter.2.cloned.1.call-update) | async-done | bytes 8208 | tf_op jit(solution)/shard_map/reduce_scatter | solution.py:58
  583.5 1.3 multiply_reduce_fusion
  584.8 252.2 %psum.28 = f32[]{:T(128)} all-reduce(f32[]{:T(128)} %multiply_reduce_fusion), channel_id=1, replica_groups=mesh['layer'=4,'expert'=128] {'expert'}, use_global_device_ids=true, to_apply=%region_7.8 | all-reduce | flops 1 | bytes 8 | tf_op jit(solution)/shard_map/psum | solution.py:59
  837.8 1.7 fusion.36
  839.5 0.0 all-reduce.5.cloned.1.call-update
  839.5 0.0 all-reduce.7.cloned.1.call-start
  839.5 178.0 %all-reduce.5.cloned.1.call-done = f32[128,128]{1,0:T(8,128)} async-done(((f32[128,128]{1,0:T(8,128)}), f32[128,128]{1,0:T(8,128)}) %all-reduce.5.cloned.1.call-update) | async-done | bytes 65552 | tf_op jit(solution)/shard_map/psum | solution.py:54
  1017.6 1.2 fusion.22
  1018.7 0.9 convolution_add_fusion.2
  1019.7 0.9 fusion.38
  1020.6 0.0 all-reduce.7.cloned.1.call-update
  1020.6 0.0 all-reduce.9.cloned.1.call-start
  1020.7 177.2 %all-reduce.7.cloned.1.call-done = f32[128,128]{1,0:T(8,128)} async-done(((f32[128,128]{1,0:T(8,128)}), f32[128,128]{1,0:T(8,128)}) %all-reduce.7.cloned.1.call-update) | async-done | bytes 65552 | tf_op jit(solution)/shard_map/psum | solution.py:54
  1197.9 1.2 fusion.21
  1199.1 0.2 convolution_add_fusion.1
  1199.2 0.9 fusion.39
  1200.2 177.9 %all-reduce.9.cloned.1.call-done = f32[128,128]{1,0:T(8,128)} async-done(((f32[128,128]{1,0:T(8,128)}), f32[128,128]{1,0:T(8,128)}) %all-reduce.9.cloned.1.call-update) | async-done | bytes 65552 | tf_op jit(solution)/shard_map/psum | solution.py:54
  1378.1 1.2 fusion.20
  1379.3 0.8 fusion.37
  1380.1 48.2 %all_gather.7 = bf16[2048,128]{1,0:T(8,128)(2,1)S(1)} all-gather(bf16[16,128]{1,0:T(8,128)(2,1)S(1)} %get-tuple-element.6), channel_id=1, replica_groups=mesh['layer'=4,'expert'=128] {'expert'}, dimensions={0}, use_global_device_ids=true | all-gather | bytes 528384 | tf_op jit(solution)/shard_map/all_gather | solution.py:83
  1428.3 1.2 fusion.17
  1429.5 0.8 copy.12
  (17 shorter events, 0.1 us)
Async XLA Ops:
  7.2 368.4 %copy-start = (bf16[1,768,2048]{2,1,0:T(8,128)(2,1)S(1)}, bf16[1,768,2048]{2,1,0:T(8,128)(2,1)}, u32[]{:S(2)}) copy-start(bf16[1,768,2048]{2,1,0:T(8,128)(2,1)} %param.7) | copy-start | bytes 9437188
  9.3 0.8 copy-start.1
  42.9 19.1 %copy-start.2 = (f32[16,128]{1,0:T(8,128)S(1)}, f32[16,128]{1,0:T(8,128)}, u32[]{:S(2)}) copy-start(f32[16,128]{1,0:T(8,128)} %param.6) | copy-start | bytes 24580
  42.9 312.4 %all-to-all-start = ((bf16[128,10,2048]{2,1,0:T(8,128)(2,1)}), bf16[128,10,2048]{2,1,0:T(8,128)(2,1)}, u32[]{:S(2)}, u32[]{:S(2)}) async-start(bf16[128,10,2048]{2,1,0:T(8,128)(2,1)} %reshape.102), calls=%async_computation | async-start | bytes 16777216 | tf_op jit(solution)/shard_map/all_to_all | solution.py:79
  61.9 521.7 %reduce-scatter.2.cloned.1.call-start = ((), (), s32[]{:S(2)}) async-start(), calls=%async_computation.2 | async-start | bytes 1056768 | tf_op jit(solution)/shard_map/reduce_scatter | solution.py:58
  390.0 627.6 %all-reduce.5.cloned.1.call-start = ((), (), s32[]{:S(2)}) async-start(), calls=%async_computation.3 | async-start | bytes 131072 | tf_op jit(solution)/shard_map/psum | solution.py:54
  839.5 358.4 %all-reduce.7.cloned.1.call-start = ((), (), s32[]{:S(2)}) async-start(), calls=%async_computation.4 | async-start | bytes 131072 | tf_op jit(solution)/shard_map/psum | solution.py:54
  1020.6 357.5 %all-reduce.9.cloned.1.call-start = ((), (), s32[]{:S(2)}) async-start(), calls=%async_computation.5 | async-start | bytes 131072 | tf_op jit(solution)/shard_map/psum | solution.py:54
Sparse Core Ops, SparseCore 0:
  390.1 193.3 reduce-scatter.1
  839.6 177.9 all-reduce.4
  1021.4 176.4 all-reduce.6
  1201.6 176.4 all-reduce.8
where the time goes:
time: 1440 us
  waiting for transfers between devices  727 us (50%)
  blocking collectives  594 us (41%)
  local copies, waits for them, and re-layouts  40.6 us (3%)
  matrix products  34.8 us (2%)
  starting transfers between devices  19.2 us (1%)
  between operations  14.6 us (1%)
    psum x3, waiting for transfers between devices, share_gram(): return lax.psum(local_gram, 'expert')  533 us
    all_gather x1, blocking collectives, shards(): lax.all_gather(start_basis.astype(jnp.bfloat16), 'expert', axis=0, tiled=...  293 us
    psum x1, blocking collectives, ortho_rows(): power = lax.psum(jnp.sum(shard * shard), 'expert') + epsilon  252 us
    reduce_scatter x1, waiting for transfers between devices, ortho_rows(): shard = lax.psum_scatter(term, 'expert', scatter_dimension=0, tiled=True)  193 us
    all_gather x1, blocking collectives, shards(): lax.all_gather(local.astype(jnp.bfloat16), 'expert', axis=0, tiled=True)  48.2 us
  transfers between devices with their start and end apart: 5, of which 4 were waited for; matrix products, arithmetic and copies ran while one was open for 0% of the time, Pallas kernels for 0%

commit v1 on v0

v1 whole, which is shorter than its diff:
```python
import jax
import jax.numpy as jnp
from jax import lax
from jax.sharding import PartitionSpec as P

NS_STEPS = 3
MAIN = 8

epsilon = 1e-06
coef_a = 3.4445
coef_b = -4.775
coef_c = 2.0315
HI = lax.Precision.HIGHEST


def dot(a, b):
    return jnp.dot(a, b, preferred_element_type=jnp.float32)


def dot_t(a, b):
    return lax.dot_general(a, b, (((0,), (0,)), ((), ())), preferred_element_type=jnp.float32)


def slot_rank(block_ids, experts):
    row_count = block_ids.shape[0]
    names = jnp.arange(experts, dtype=jnp.int32)[:, None, None]
    member = jnp.any(block_ids[None, :, :] == names, axis=2).astype(jnp.bfloat16)
    index = jnp.arange(row_count, dtype=jnp.int32)
    ahead = (index[:, None] <= index[None, :]).astype(jnp.bfloat16)
    rank = jnp.dot(member, ahead, preferred_element_type=jnp.float32)
    return jnp.where(member > 0, rank, 0.0)


def pick(rank, normed, first, count):
    wanted = jnp.arange(first + 1, first + count + 1).astype(jnp.float32)
    chosen = (rank[:, None, :] == wanted[None, :, None]).astype(jnp.bfloat16)
    chosen = chosen.reshape(rank.shape[0] * count, rank.shape[1])
    return dot(chosen, normed).astype(jnp.bfloat16)


def ortho(total, own):
    power = jnp.sum(total * total) + epsilon
    scale = 1.0 / jnp.sqrt(power)
    current = total * scale
    eye = jnp.eye(total.shape[1], dtype=jnp.float32)
    gram = jnp.dot(current.T, current, precision=HI)
    product = None
    for step in range(NS_STEPS):
        square = jnp.dot(gram, gram, precision=HI)
        factor = coef_a * eye + coef_b * gram + coef_c * square
        product = factor if product is None else jnp.dot(product, factor, precision=HI)
        if step + 1 < NS_STEPS:
            gram = jnp.dot(jnp.dot(factor, gram, precision=HI), factor, precision=HI)
    return jnp.dot(current, product, precision=HI), jnp.dot(own * scale, product, precision=HI)


def shards(rows, expert_ids, start_basis, weights):
    row_count, width = rows.shape
    rank_width = start_basis.shape[1]
    share = start_basis.shape[0]
    group = lax.axis_size("expert")
    experts = group * weights.shape[0]
    capacity = max(2, min(row_count, row_count * expert_ids.shape[1] * 5 // (4 * experts)))
    spare = capacity - MAIN
    weight = weights[0]
    values = rows.astype(jnp.float32)
    power = jnp.mean(values * values, axis=1, keepdims=True) + epsilon
    normed = (values / jnp.sqrt(power)).astype(jnp.bfloat16)
    rank = slot_rank(expert_ids, experts)
    main = pick(rank, normed, 0, MAIN).reshape(experts, MAIN, width)
    rest = pick(rank, normed, MAIN, spare).reshape(experts, spare * width // rank_width, rank_width)
    basis_rows = jnp.broadcast_to(start_basis.astype(jnp.bfloat16), (experts, share, rank_width))
    second = jnp.concatenate([rest, basis_rows], axis=1)
    second = lax.all_to_all(second, "expert", split_axis=0, concat_axis=0, tiled=True)
    main = lax.all_to_all(main, "expert", split_axis=0, concat_axis=0, tiled=True)
    cut = spare * width // rank_width
    basis_bf = second[:, cut:, :].reshape(group * share, rank_width)
    x_rest = second[:, :cut, :].reshape(group * spare, width)
    x_main = main.reshape(group * MAIN, width)
    bf = jnp.bfloat16
    a_main = dot(x_main, basis_bf).astype(bf)
    a_rest = dot(x_rest, basis_bf).astype(bf)
    b = (dot_t(x_main, a_main) + dot_t(x_rest, a_rest)).astype(bf)
    c = dot(weight, b).astype(bf)
    e = dot_t(weight, c).astype(bf)
    f_main = dot(x_main, e).astype(bf)
    f_rest = dot(x_rest, e).astype(bf)
    term = dot_t(x_main, f_main) + dot_t(x_rest, f_rest)
    parts = lax.all_to_all(term.reshape(group, share, rank_width), "expert", split_axis=0, concat_axis=0, tiled=True)
    own = jnp.sum(parts, axis=0)
    spread = jnp.broadcast_to(own[None], (group, share, rank_width))
    total = lax.all_to_all(spread, "expert", split_axis=0, concat_axis=0, tiled=True).reshape(group * share, rank_width)
    whole, local = ortho(total, own)
    compressed = dot(weight, whole.astype(bf)).astype(bf)
    return (compressed[None], local)


def solution(mesh):
    in_specs = (
        P(("layer", "expert"), None),
        P(("layer", "expert"), None),
        P(("layer", "expert"), None),
        P(("layer", "expert"), None, None),
    )
    out_specs = (P(("layer", "expert"), None, None), P(("layer", "expert"), None))
    return jax.shard_map(shards, mesh=mesh, in_specs=in_specs, out_specs=out_specs, check_vma=False)
```

time: 1440 us -> 304 us (0.21)
  waiting for transfers between devices: 727 us -> 122 us
  blocking collectives: 594 us -> 89.1 us
  local copies, waits for them, and re-layouts: 40.6 us -> 11.7 us
    psum x3 -> x0, waiting for transfers between devices: 533 us -> none  [share_gram(): return lax.psum(local_gram, 'expert')]
    all_gather x2 -> x0, blocking collectives: 342 us -> none  [the longest x1 293 us: shards(): lax.all_gather(start_basis.astype(jnp.bfloat16), 'expert', axis=0, tiled=...]
    psum x1 -> x0, blocking collectives: 252 us -> none  [ortho_rows(): power = lax.psum(jnp.sum(shard * shard), 'expert') + epsilon]
    reduce_scatter x1 -> x0, waiting for transfers between devices: 193 us -> none  [ortho_rows(): shard = lax.psum_scatter(term, 'expert', scatter_dimension=0, tiled=True)]
    all_to_all x1 -> x2, waiting for transfers between devices: 0.01 us -> 122 us  [the longest x1 85.2 us: shards(): lax.all_to_all(main, 'expert', split_axis=0, concat_axis=0, tiled=True)]
    all_to_all x0 -> x2, blocking collectives: none -> 89.1 us  [the longest x1 52 us: shards(): lax.all_to_all(term.reshape(group, share, rank_width), 'expert', split_ax...]
    dot_general x13 -> x21, matrix products: 34.8 us -> 43.5 us  [the longest x5 29.9 us: dot_t(): lax.dot_general(a, b, (((0,), (0,)), ((), ())), preferred_element_type=jn...]
  transfers between devices with their start and end apart: 5 -> 2, of which waited for: 4 -> 2; matrix products, arithmetic and copies ran while one was open for 0% -> 5% of each run, Pallas kernels for 0% -> 0%
where the time goes in v1:
time: 304 us; the launch traced here: 303 us
  waiting for transfers between devices  122 us (40%)
  blocking collectives  89.1 us (29%)
  matrix products  43.5 us (14%)
  starting transfers between devices  26.8 us (9%)
  local copies, waits for them, and re-layouts  11.7 us (4%)
  other arithmetic  9.24 us (3%)
    all_to_all x1, waiting for transfers between devices, shards(): lax.all_to_all(main, 'expert', split_axis=0, concat_axis=0, tiled=True)  85.2 us
    all_to_all x1, blocking collectives, shards(): lax.all_to_all(term.reshape(group, share, rank_width), 'expert', split_ax...  52 us
    all_to_all x1, blocking collectives, shards(): lax.all_to_all(spread, 'expert', split_axis=0, concat_axis=0, tiled=True)  37.2 us
    all_to_all x1, waiting for transfers between devices, shards(): lax.all_to_all(second, 'expert', split_axis=0, concat_axis=0, tiled=True)  36.4 us
    dot_general x5, matrix products, dot_t(): lax.dot_general(a, b, (((0,), (0,)), ((), ())), preferred_element_type=jn...  29.9 us
    all_to_all x1, starting transfers between devices, shards(): lax.all_to_all(second, 'expert', split_axis=0, concat_axis=0, tiled=True)  18.8 us
    dot_general x3, matrix products, dot(): return jnp.dot(a, b, preferred_element_type=jnp.float32)  8.1 us
    all_to_all x1, starting transfers between devices, shards(): lax.all_to_all(main, 'expert', split_axis=0, concat_axis=0, tiled=True)  7.96 us
  transfers between devices with their start and end apart: 2, of which 2 were waited for; matrix products, arithmetic and copies ran while one was open for 5% of the time, Pallas kernels for 0%

profile of v1, /device:TPU:1, one launch (start us, length us, event | category | flops | bytes accessed | tf_op | source)
XLA Modules:
  0.0 303.5 jit_solution(12786053015536869594)
XLA Ops:
  0.6 0.0 copy-start
  0.7 1.4 fusion.52
  2.0 0.7 convert_element_type.75
  2.8 0.9 fusion.54
  3.6 0.1 convolution_select_fusion
  3.8 0.1 eq.72
  4.0 2.6 convolution_convert_fusion
  6.5 2.3 reshape.56
  8.9 0.1 broadcast_in_dim.11
  8.9 2.5 pad_maximum_fusion
  11.4 18.8 %all-to-all-start.1 = ((bf16[128,48,128]{2,1,0:T(8,128)(2,1)}), bf16[128,48,128]{2,1,0:T(8,128)(2,1)}, u32[]{:S(2)}, u32[]{:S(2)}) async-start(bf16[128,48,128]{2,1,0:T(8,128)(2,1)} %pad_maximum_fusion), calls=%async_computation.1 | async-start | bytes 3145728 | tf_op jit(solution)/shard_map/all_to_all | solution.py:74
  30.3 0.1 eq.66
  30.4 4.3 %convert_bitcast_fusion = bf16[128,8,2048]{2,1,0:T(8,128)(2,1)} fusion(f32[1024]{0:T(1024)S(1)} %eq.66, f32[128,128]{1,0:T(8,128)S(1)} %convolution_select_fusion, bf16[128,2048]{1,0:T(8,128)(2,1)} %param.4, f32[128]{0:T(128)S(1)} %add_sqrt_fusion), kind=kOutput, calls=%fused_computation.8 | convolution fusion | flops 539885568 | bytes 4788736 | tf_op jit(solution)/shard_map/dot_general | solution.py:17
  34.7 36.4 %all-to-all-done.1 = bf16[128,48,128]{2,1,0:T(8,128)(2,1)} async-done(((bf16[128,48,128]{2,1,0:T(8,128)(2,1)}), bf16[128,48,128]{2,1,0:T(8,128)(2,1)}, u32[]{:S(2)}, u32[]{:S(2)}) %all-to-all-start.1) | async-done | bytes 1572896 | tf_op jit(solution)/shard_map/all_to_all | solution.py:74
  71.2 8.0 %all-to-all-start = ((bf16[128,8,2048]{2,1,0:T(8,128)(2,1)}), bf16[128,8,2048]{2,1,0:T(8,128)(2,1)}, u32[]{:S(2)}, u32[]{:S(2)}) async-start(bf16[128,8,2048]{2,1,0:T(8,128)(2,1)} %convert_bitcast_fusion), calls=%async_computation | async-start | bytes 8388608 | tf_op jit(solution)/shard_map/all_to_all | solution.py:75
  79.1 2.3 slice.9
  81.4 2.3 reshape.58
  83.7 1.9 slice.8
  85.6 3.7 %fusion.47 = f32[2048,128]{1,0:T(8,128)} fusion(bf16[256,2048]{1,0:T(8,128)(2,1)} %reshape.58, bf16[2048,128]{1,0:T(8,128)(2,1)} %bitcast.89), kind=kOutput, calls=%fused_computation.31 | convolution fusion | flops 268468224 | bytes 2621440 | tf_op jit(solution)/shard_map/dot_general | solution.py:21
  89.3 85.2 %all-to-all-done = bf16[128,8,2048]{2,1,0:T(8,128)(2,1)} async-done(((bf16[128,8,2048]{2,1,0:T(8,128)(2,1)}), bf16[128,8,2048]{2,1,0:T(8,128)(2,1)}, u32[]{:S(2)}, u32[]{:S(2)}) %all-to-all-start) | async-done | bytes 4194336 | tf_op jit(solution)/shard_map/all_to_all | solution.py:75
  174.5 9.0 %fusion.20 = bf16[2048,128]{1,0:T(8,128)(2,1)} fusion(f32[2048,128]{1,0:T(8,128)} %fusion.47, bf16[128,8,2048]{2,1,0:T(8,128)(2,1)} %all-to-all-done, bf16[2048,128]{1,0:T(8,128)(2,1)} %bitcast.90), kind=kOutput, calls=%fused_computation.18 | convolution fusion | flops 1074397184 | bytes 6291456 | tf_op jit(solution)/shard_map/dot_general | solution.py:21
  183.5 0.0 copy-done
  183.5 3.9 %fusion.23 = bf16[128,2048]{1,0:T(8,128)(2,1)} fusion(bf16[1,768,2048]{2,1,0:T(8,128)(2,1)S(1)} %copy-done, bf16[2048,128]{1,0:T(8,128)(2,1)} %fusion.20), kind=kOutput, calls=%fused_computation.19 | convolution fusion | flops 805666816 | bytes 4194304 | tf_op jit(solution)/shard_map/dot_general | solution.py:21
  187.4 4.1 %fusion.48 = f32[2048,128]{1,0:T(8,128)} fusion(bf16[256,2048]{1,0:T(8,128)(2,1)} %reshape.58, bf16[128,2048]{1,0:T(8,128)(2,1)} %fusion.23), kind=kOutput, calls=%fused_computation.32 | convolution fusion | flops 268468224 | bytes 2621440 | tf_op jit(solution)/shard_map/dot_general | solution.py:21
  191.5 9.2 %fusion.17 = f32[2048,128]{1,0:T(8,128)} fusion(f32[2048,128]{1,0:T(8,128)} %fusion.48, bf16[128,8,2048]{2,1,0:T(8,128)(2,1)} %all-to-all-done, bf16[128,2048]{1,0:T(8,128)(2,1)} %fusion.23), kind=kOutput, calls=%fused_computation.17 | convolution fusion | flops 1074135040 | bytes 6815744 | tf_op jit(solution)/shard_map/dot_general | solution.py:21
  200.7 52.0 %all_to_all.20 = f32[128,16,128]{2,1,0:T(8,128)} all-to-all(f32[128,16,128]{2,1,0:T(8,128)} %bitcast.92), channel_id=1, replica_groups=mesh['layer'=4,'expert'=128] {'expert'}, dimensions={0} | all-to-all | bytes 2097152 | tf_op jit(solution)/shard_map/all_to_all | solution.py:89
  252.7 1.4 reduce_sum.28
  254.0 0.1 broadcast_in_dim.12
  254.1 37.2 %all_to_all.21 = f32[128,16,128]{2,1,0:T(8,128)S(1)} all-to-all(f32[128,16,128]{2,1,0:T(8,128)S(1)} %broadcast_in_dim.12), channel_id=1, replica_groups=mesh['layer'=4,'expert'=128] {'expert'}, dimensions={0} | all-to-all | bytes 2097152 | tf_op jit(solution)/shard_map/all_to_all | solution.py:92
  291.3 0.0 copy-start.1
  291.3 1.0 copy-done.1
  292.3 0.9 multiply_reduce_fusion
  293.8 1.6 copy_multiply_fusion
  295.4 1.8 convolution_bitcast_fusion
  297.2 0.6 copy.19
  297.8 0.2 fusion.51
  298.0 0.2 fusion.64
  298.3 0.2 fusion.65
  298.5 0.2 fusion.50
  298.7 0.2 fusion.67
  298.9 0.2 fusion.66
  299.1 0.2 fusion.68
  299.3 0.2 fusion.49
  299.5 0.2 fusion.69
  299.7 0.8 fusion.59
  300.5 1.0 convolution_convert_fusion.1
  301.5 1.2 fusion.44
  302.7 0.8 copy.21
  (6 shorter events, 0.1 us)
Async XLA Ops:
  0.6 182.9 %copy-start = (bf16[1,768,2048]{2,1,0:T(8,128)(2,1)S(1)}, bf16[1,768,2048]{2,1,0:T(8,128)(2,1)}, u32[]{:S(2)}) copy-start(bf16[1,768,2048]{2,1,0:T(8,128)(2,1)} %param.7) | copy-start | bytes 9437188
  11.4 59.7 %all-to-all-start.1 = ((bf16[128,48,128]{2,1,0:T(8,128)(2,1)}), bf16[128,48,128]{2,1,0:T(8,128)(2,1)}, u32[]{:S(2)}, u32[]{:S(2)}) async-start(bf16[128,48,128]{2,1,0:T(8,128)(2,1)} %pad_maximum_fusion), calls=%async_computation.1 | async-start | bytes 3145728 | tf_op jit(solution)/shard_map/all_to_all | solution.py:74
  71.2 103.4 %all-to-all-start = ((bf16[128,8,2048]{2,1,0:T(8,128)(2,1)}), bf16[128,8,2048]{2,1,0:T(8,128)(2,1)}, u32[]{:S(2)}, u32[]{:S(2)}) async-start(bf16[128,8,2048]{2,1,0:T(8,128)(2,1)} %convert_bitcast_fusion), calls=%async_computation | async-start | bytes 8388608 | tf_op jit(solution)/shard_map/all_to_all | solution.py:75
  291.3 1.0 copy-start.1

commit v2 on v1

v2 whole, which is shorter than its diff:
```python
import jax
import jax.numpy as jnp
from jax import lax
from jax.experimental import pallas as pl
from jax.experimental.pallas import tpu as pltpu
from jax.sharding import Mesh, PartitionSpec as P

NS_STEPS = 3
MAIN = 8
LANES = 128
STEP = 16

epsilon = 1e-06
coef_a = 3.4445
coef_b = -4.775
coef_c = 2.0315
HI = lax.Precision.HIGHEST
BF = jnp.bfloat16
F32 = jnp.float32


def iota(shape, axis):
    return lax.broadcasted_iota(jnp.int32, shape, axis)


def dot(a, b, contract=((1,), (0,)), precision=None):
    return lax.dot_general(a, b, (contract, ((), ())), precision=precision, preferred_element_type=F32)


def as_bf16(flag):
    return jnp.where(flag, 1.0, 0.0).astype(BF)


def pack_kernel(main_steps, spare, ids_ref, rows_ref, basis_ref, out_ref, normed_ref, rank_ref, pick_ref, fan_ref):
    step = pl.program_id(0)
    tops, row_count = ids_ref.shape
    experts = out_ref.shape[0]

    @pl.when(step == 0)
    def _():
        values = rows_ref[...].astype(F32)
        power = jnp.mean(values * values, axis=1, keepdims=True) + epsilon
        normed = (values / jnp.sqrt(power)).astype(BF)
        for t in range(main_steps):
            normed_ref[t] = normed[:, 2 * LANES * t:2 * LANES * (t + 1)]
        member = jnp.zeros((experts, row_count), F32)
        for top in range(tops):
            named = jnp.broadcast_to(ids_ref[top:top + 1, :], (experts, row_count))
            member = member + jnp.where(named == iota((experts, row_count), 0), 1.0, 0.0)
        ahead = as_bf16(iota((row_count, row_count), 0) <= iota((row_count, row_count), 1))
        rank = jnp.where(member > 0.0, dot(member.astype(BF), ahead), 0.0)
        rank_ref[...] = rank
        slots = experts * MAIN
        owner = as_bf16(iota((slots, experts), 0) // MAIN == iota((slots, experts), 1))
        wanted = (iota((slots, row_count), 0) % MAIN + 1).astype(F32)
        pick_ref[...] = as_bf16(dot(owner, rank.astype(BF)) == wanted)

    @pl.when(step < main_steps)
    def _():
        both = dot(pick_ref[...], normed_ref[step]).astype(BF)
        out_ref[:, 0:MAIN, :] = both[:, :LANES].reshape(experts, MAIN, LANES)
        out_ref[:, MAIN:, :] = both[:, LANES:].reshape(experts, MAIN, LANES)

    @pl.when((step >= main_steps) & (step < main_steps + spare))
    def _():
        wanted = (step - main_steps + MAIN + 1).astype(F32)
        pick = as_bf16(rank_ref[...] == wanted)
        for t in range(main_steps):
            both = dot(pick, normed_ref[t])
            fan_ref[pl.ds(2 * t, experts, stride=STEP), :] = both[:, :LANES]
            fan_ref[pl.ds(2 * t + 1, experts, stride=STEP), :] = both[:, LANES:]
        out_ref[...] = fan_ref[...].reshape(experts, STEP, LANES).astype(BF)

    @pl.when(step == main_steps + spare)
    def _():
        basis = basis_ref[...].astype(BF)
        out_ref[...] = jnp.broadcast_to(basis[None], out_ref.shape)


def pack(ids_t, rows, basis, experts, spare):
    row_count, width = rows.shape
    main_steps = width // (2 * LANES)
    steps = main_steps + spare + 1
    return pl.pallas_call(
        lambda *refs: pack_kernel(main_steps, spare, *refs),
        grid=(steps,),
        out_shape=jax.ShapeDtypeStruct((experts, STEP * steps, LANES), BF),
        in_specs=[
            pl.BlockSpec(ids_t.shape, lambda i: (0, 0)),
            pl.BlockSpec(rows.shape, lambda i: (0, 0)),
            pl.BlockSpec(basis.shape, lambda i: (0, 0)),
        ],
        out_specs=pl.BlockSpec((experts, STEP, LANES), lambda i: (0, i, 0)),
        scratch_shapes=[
            pltpu.VMEM((main_steps, row_count, 2 * LANES), BF),
            pltpu.VMEM((experts, row_count), F32),
            pltpu.VMEM((experts * MAIN, row_count), BF),
            pltpu.VMEM((experts * STEP, LANES), F32),
        ],
        name="pack",
    )(ids_t, rows, basis)


def chain_kernel(main_steps, spare, core_ref, got_ref, weight_ref, keep_ref, send_ref, buf, x, w, fan, y, sems, w_sem):
    steps = main_steps + spare + 1
    group = got_ref.shape[0]
    core = core_ref[0]
    copies = [
        pltpu.make_async_copy(got_ref.at[:, pl.ds(STEP * i, STEP), :], buf.at[i], sems.at[i]) for i in range(steps)
    ]
    load_w = pltpu.make_async_copy(weight_ref, w, w_sem)
    order = [steps - 1] + list(range(main_steps, main_steps + spare)) + list(range(main_steps))
    for i in order:
        copies[i].start()
    load_w.start()
    copies[steps - 1].wait()
    basis = buf[steps - 1].reshape(group * STEP, LANES)
    main = group * MAIN
    for k in range(spare):
        copies[main_steps + k].wait()
        fan[...] = buf[main_steps + k].reshape(group * STEP, LANES).astype(F32)
        for j in range(STEP):
            x[pl.ds(main + group * k, group), LANES * j:LANES * (j + 1)] = fan[
                pl.ds(j, group, stride=STEP), :
            ].astype(BF)
    first = None
    for t in range(main_steps):
        copies[t].wait()
        at = 2 * LANES * t
        x[0:main, at:at + LANES] = buf[t, :, 0:MAIN, :].reshape(main, LANES)
        x[0:main, at + LANES:at + 2 * LANES] = buf[t, :, MAIN:, :].reshape(main, LANES)
        part = dot(x[:, at:at + 2 * LANES], basis[at:at + 2 * LANES, :])
        first = part if first is None else first + part
    rows = x[...]
    second = dot(first.astype(BF), rows, ((0,), (0,))).astype(BF)
    load_w.wait()
    weight = w[...]
    inner = dot(second, weight, ((1,), (1,))).astype(BF)
    back = dot(inner, weight).astype(BF)
    again = dot(rows, back, ((1,), (1,))).astype(BF)
    term = dot(again, rows, ((0,), (0,)))
    y[...] = term.T.reshape(y.shape)
    keep_ref[...] = y[:, core]
    send_ref[...] = y[:, 1 - core]


def chain(core, got, weight, spare):
    group = got.shape[0]
    width = weight.shape[1]
    main_steps = width // (2 * LANES)
    steps = main_steps + spare + 1
    half = jax.ShapeDtypeStruct((group // 2, STEP, LANES), F32)
    vmem = pl.BlockSpec(memory_space=pltpu.VMEM)
    hbm = pl.BlockSpec(memory_space=pl.ANY)
    return pl.pallas_call(
        lambda *refs: chain_kernel(main_steps, spare, *refs),
        out_shape=(half, half),
        in_specs=[pl.BlockSpec(memory_space=pltpu.SMEM), hbm, hbm],
        out_specs=(vmem, vmem),
        scratch_shapes=[
            pltpu.VMEM((steps, group, STEP, LANES), BF),
            pltpu.VMEM((group * (MAIN + spare), width), BF),
            pltpu.VMEM(weight.shape, BF),
            pltpu.VMEM((group * STEP, LANES), F32),
            pltpu.VMEM((group // 2, 2, STEP, LANES), F32),
            pltpu.SemaphoreType.DMA((steps,)),
            pltpu.SemaphoreType.DMA,
        ],
        name="chain",
    )(core, got, weight)


def ortho_kernel(core_ref, mine_ref, other_ref, own_ref, weight_ref, packed_ref, local_ref, z, w, w_sem):
    core = core_ref[0]
    load_w = pltpu.make_async_copy(weight_ref, w, w_sem)
    load_w.start()
    z[:, core] = mine_ref[...]
    z[:, 1 - core] = other_ref[...]
    size = z.shape[0] * z.shape[1] * z.shape[2]
    total = z[...].reshape(size, LANES)
    raw = dot(total, total, ((0,), (0,)), HI)
    diagonal = iota((LANES, LANES), 0) == iota((LANES, LANES), 1)
    eye = jnp.where(diagonal, 1.0, 0.0)
    power = jnp.sum(jnp.where(diagonal, raw, 0.0), keepdims=True) + epsilon
    scale = 1.0 / jnp.sqrt(power)
    gram = (raw * scale) * scale
    product = None
    for step in range(NS_STEPS):
        factor = coef_a * eye + coef_b * gram + coef_c * dot(gram, gram, precision=HI)
        product = factor if product is None else dot(product, factor, precision=HI)
        if step + 1 < NS_STEPS:
            gram = dot(dot(factor, gram, precision=HI), factor, precision=HI)
    whole = dot(total * scale, product, precision=HI)
    local_ref[...] = dot(own_ref[...] * scale, product, precision=HI)
    load_w.wait()
    packed_ref[...] = dot(w[...], whole.astype(BF)).astype(BF)


def ortho(core, mine, other, own, weight):
    vmem = pl.BlockSpec(memory_space=pltpu.VMEM)
    return pl.pallas_call(
        ortho_kernel,
        out_shape=(
            jax.ShapeDtypeStruct((weight.shape[0], LANES), BF),
            jax.ShapeDtypeStruct(own.shape, F32),
        ),
        in_specs=[pl.BlockSpec(memory_space=pltpu.SMEM), vmem, vmem, vmem, pl.BlockSpec(memory_space=pl.ANY)],
        out_specs=(vmem, vmem),
        scratch_shapes=[
            pltpu.VMEM((mine.shape[0], 2) + mine.shape[1:], F32),
            pltpu.VMEM(weight.shape, BF),
            pltpu.SemaphoreType.DMA,
        ],
        name="ortho",
    )(core, mine, other, own, weight)


def shards(rows, expert_ids, start_basis, weights):
    row_count = rows.shape[0]
    experts = lax.axis_size("chip") * lax.axis_size("core") * weights.shape[0]
    capacity = max(2, min(row_count, row_count * expert_ids.shape[1] * 5 // (4 * experts)))
    spare = capacity - MAIN
    weight = weights[0]
    core = lax.axis_index("core").astype(jnp.int32).reshape(1)
    swap = [(0, 1), (1, 0)]
    sent = pack(expert_ids.T, rows, start_basis, experts, spare)
    got = lax.all_to_all(sent, ("chip", "core"), split_axis=0, concat_axis=0, tiled=True)
    keep, send = chain(core, got, weight, spare)
    half = keep + lax.ppermute(send, "core", swap)
    parts = lax.all_to_all(half, "chip", split_axis=0, concat_axis=0, tiled=True)
    own = jnp.sum(parts, axis=0)
    spread = jnp.broadcast_to(own[None], parts.shape)
    mine = lax.all_to_all(spread, "chip", split_axis=0, concat_axis=0, tiled=True)
    other = lax.ppermute(mine, "core", swap)
    compressed, local = ortho(core, mine, other, own, weight)
    return (compressed[None], local)


def solution(mesh):
    layers, members = mesh.devices.shape
    inner = Mesh(mesh.devices.reshape(layers, members // 2, 2), ("layer", "chip", "core"))
    split = ("layer", "chip", "core")
    in_specs = (P(split, None), P(split, None), P(split, None), P(split, None, None))
    out_specs = (P(split, None, None), P(split, None))
    return jax.shard_map(shards, mesh=inner, in_specs=in_specs, out_specs=out_specs, check_vma=False)
```

time: 304 us -> 273 us (0.90)
  matrix products: 43.5 us -> 0 us
  Pallas kernels: 0 us -> 31.4 us
  blocking collectives: 89.1 us -> 64.5 us
  waiting for transfers between devices: 122 us -> 146 us
  local copies, waits for them, and re-layouts: 11.7 us -> 0.84 us
  other arithmetic: 9.24 us -> 1.18 us
    dot_general x21 -> x0, matrix products: 43.5 us -> none  [the longest x5 29.9 us: dot_t(): lax.dot_general(a, b, (((0,), (0,)), ((), ())), preferred_element_type=jn...]
    pallas_call x0 -> x3, Pallas kernels: none -> 31.4 us  [the longest x1 14.8 us: chain(): pl.pallas_call(lambda *refs: chain_kernel(main_steps, spare, *refs), out_...]
    all_to_all x2, blocking collectives: 89.1 us -> 64.5 us  [the longest x1 41.4 us: shards(): lax.all_to_all(half, 'chip', split_axis=0, concat_axis=0, tiled=True)]
    all_to_all x2 -> x1, waiting for transfers between devices: 122 us -> 143 us  [shards(): lax.all_to_all(sent, ('chip', 'core'), split_axis=0, concat_axis=0, tiled...]
    ppermute x0 -> x2, starting transfers between devices: none -> 8.98 us  [the longest x1 5.81 us: shards(): other = lax.ppermute(mine, 'core', swap)]
    all_to_all x2 -> x1, starting transfers between devices: 26.8 us -> 18.8 us  [shards(): lax.all_to_all(sent, ('chip', 'core'), split_axis=0, concat_axis=0, tiled...]
    reshape x2 -> x0, local copies, waits for them, and re-layouts: 4.66 us -> none  [the longest x1 2.33 us: shards(): pick(rank, normed, MAIN, spare)]
    slice x2 -> x0, local copies, waits for them, and re-layouts: 4.17 us -> none  [the longest x1 2.27 us: shards(): x_rest = second[:, :cut, :].reshape(group * spare, width)]
  transfers between devices with their start and end apart: 2 -> 3, of which waited for: 2 -> 3; matrix products, arithmetic and copies ran while one was open for 5% -> 0% of each run, Pallas kernels for 0% -> 0%
where the time goes in v2:
time: 273 us
  waiting for transfers between devices  146 us (53%)
  blocking collectives  64.5 us (24%)
  Pallas kernels  31.4 us (12%)
  starting transfers between devices  27.8 us (10%)
    all_to_all x1, waiting for transfers between devices, shards(): lax.all_to_all(sent, ('chip', 'core'), split_axis=0, concat_axis=0, tiled...  143 us
    all_to_all x1, blocking collectives, shards(): lax.all_to_all(half, 'chip', split_axis=0, concat_axis=0, tiled=True)  41.4 us
    all_to_all x1, blocking collectives, shards(): lax.all_to_all(spread, 'chip', split_axis=0, concat_axis=0, tiled=True)  23.1 us
    all_to_all x1, starting transfers between devices, shards(): lax.all_to_all(sent, ('chip', 'core'), split_axis=0, concat_axis=0, tiled...  18.8 us
    pallas_call x1, Pallas kernels, chain(): pl.pallas_call(lambda *refs: chain_kernel(main_steps, spare, *refs), out_...  14.8 us
    pallas_call x1, Pallas kernels, pack(): pl.pallas_call(lambda *refs: pack_kernel(main_steps, spare, *refs), grid=...  8.36 us
    pallas_call x1, Pallas kernels, ortho(): pl.pallas_call(ortho_kernel, out_shape=(jax.ShapeDtypeStruct((weight.shap...  8.28 us
    ppermute x1, starting transfers between devices, shards(): other = lax.ppermute(mine, 'core', swap)  5.81 us
  transfers between devices with their start and end apart: 3, of which 3 were waited for; matrix products, arithmetic and copies ran while one was open for 0% of the time, Pallas kernels for 0%

profile of v2, /device:TPU:1, one launch (start us, length us, event | category | flops | bytes accessed | tf_op | source)
XLA Modules:
  0.0 272.6 jit_solution(3971978231236010851)
XLA Ops:
  0.6 8.4 %pack.1 = bf16[128,176,128]{2,1,0:T(8,128)(2,1)} custom-call(s32[8,128]{1,0:T(8,128)} %bitcast.6, bf16[128,2048]{1,0:T(8,128)(2,1)} %refs_1_.1, f32[16,128]{1,0:T(8,128)} %refs_2_.1), custom_call_target="tpu_custom_call" | custom-call | tf_op jit(solution)/shard_map/pack/pallas_call | solution.py:84
  9.0 18.8 %all-to-all-start = ((bf16[128,176,128]{2,1,0:T(8,128)(2,1)}), bf16[128,176,128]{2,1,0:T(8,128)(2,1)}, u32[]{:S(2)}, u32[]{:S(2)}) async-start(bf16[128,176,128]{2,1,0:T(8,128)(2,1)} %pack.1), calls=%async_computation | async-start | bytes 11534336 | tf_op jit(solution)/shard_map/all_to_all | solution.py:227
  27.8 142.8 %all-to-all-done.refs_1_ = bf16[128,176,128]{2,1,0:T(8,128)(2,1)} async-done(((bf16[128,176,128]{2,1,0:T(8,128)(2,1)}), bf16[128,176,128]{2,1,0:T(8,128)(2,1)}, u32[]{:S(2)}, u32[]{:S(2)}) %all-to-all-start) | async-done | bytes 5767200 | tf_op jit(solution)/shard_map/all_to_all | solution.py:227
  170.6 14.8 %chain.1 = (f32[64,16,128]{2,1,0:T(8,128)}, f32[64,16,128]{2,1,0:T(8,128)}) custom-call(s32[1]{0:T(128)} %bitcast.refs_0_.core_ref, bf16[128,176,128]{2,1,0:T(8,128)(2,1)} %all-to-all-done.refs_1_, bf16[768,2048]{1,0:T(8,128)(2,1)} %bitcast.4), custom_call_target="tpu_custom_call" | custom-call | tf_op jit(solution)/shard_map/chain/pallas_call | solution.py:155
  185.4 3.2 %collective-permute-start = (f32[64,16,128]{2,1,0:T(8,128)}, f32[64,16,128]{2,1,0:T(8,128)S(1)}, u32[]{:S(2)}, u32[]{:S(2)}) collective-permute-start(f32[64,16,128]{2,1,0:T(8,128)} %get-tuple-element.7), channel_id=1, source_target_pairs={{0,1},{1,0},{2,3},{3,2},{4,5},{5,4},{6,7},{7,6},{8,9},{9,8},{10,11... | collective-permute-start | bytes 1572872 | tf_op jit(solution)/shard_map/ppermute | solution.py:229
  188.6 1.7 collective-permute-done
  190.3 1.1 add.3
  191.4 41.4 %all_to_all.15 = f32[64,16,128]{2,1,0:T(8,128)S(1)} all-to-all(f32[64,16,128]{2,1,0:T(8,128)S(1)} %add.3), channel_id=1, replica_groups=mesh['layer'=4,'chip'=64,'core'=2] {'chip'}, dimensions={0} | all-to-all | bytes 1048576 | tf_op jit(solution)/shard_map/all_to_all | solution.py:230
  232.9 0.1 reduce_sum.9.own_ref
  232.9 0.0 copy-start.2
  233.0 23.1 %all_to_all.16.mine_ref = f32[64,16,128]{2,1,0:T(8,128)S(1)} all-to-all(f32[64,16,128]{2,1,0:T(8,128)S(1)} %broadcast_in_dim.4), channel_id=1, replica_groups=mesh['layer'=4,'chip'=64,'core'=2] {'chip'}, dimensions={0} | all-to-all | bytes 1048576 | tf_op jit(solution)/shard_map/all_to_all | solution.py:233
  256.1 0.0 copy-start
  256.1 5.8 %collective-permute-start.1 = (f32[64,16,128]{2,1,0:T(8,128)S(1)}, f32[64,16,128]{2,1,0:T(8,128)S(1)}, u32[]{:S(2)}, u32[]{:S(2)}) collective-permute-start(f32[64,16,128]{2,1,0:T(8,128)S(1)} %all_to_all.16.mine_ref), channel_id=1, source_target_pairs={{0,1},{1,0},{2,3},{3,2},{4,5},{5,4},{6,7},{7,6},{8,9},{9,8},{10,11... | collective-permute-start | bytes 1572872 | tf_op jit(solution)/shard_map/ppermute | solution.py:234
  261.9 1.5 collective-permute-done.1.other_ref
  263.4 0.0 copy-done.2
  263.4 0.0 copy-done
  263.4 0.0 copy-start.1
  263.4 0.8 copy-done.1
  264.2 8.3 %ortho.1 = (bf16[768,128]{1,0:T(8,128)(2,1)}, f32[16,128]{1,0:T(8,128)}) custom-call(s32[1]{0:T(128)} %bitcast.refs_0_.core_ref, f32[64,16,128]{2,1,0:T(8,128)} %copy-done, f32[64,16,128]{2,1,0:T(8,128)} %copy-done.1, f32[16,128]{1,0:T(8,128)} %copy-done.2, bf16[768,2048]{1,0:T(8,128)(2,1)} %bitcast.5), custom_call_target="tpu_custom_call" | custom-call | tf_op jit(solution)/shard_map/ortho/pallas_call | solution.py:201
  (1 shorter events, 0.0 us)
Async XLA Ops:
  9.0 161.6 %all-to-all-start = ((bf16[128,176,128]{2,1,0:T(8,128)(2,1)}), bf16[128,176,128]{2,1,0:T(8,128)(2,1)}, u32[]{:S(2)}, u32[]{:S(2)}) async-start(bf16[128,176,128]{2,1,0:T(8,128)(2,1)} %pack.1), calls=%async_computation | async-start | bytes 11534336 | tf_op jit(solution)/shard_map/all_to_all | solution.py:227
  185.4 4.9 %collective-permute-start = (f32[64,16,128]{2,1,0:T(8,128)}, f32[64,16,128]{2,1,0:T(8,128)S(1)}, u32[]{:S(2)}, u32[]{:S(2)}) collective-permute-start(f32[64,16,128]{2,1,0:T(8,128)} %get-tuple-element.7), channel_id=1, source_target_pairs={{0,1},{1,0},{2,3},{3,2},{4,5},{5,4},{6,7},{7,6},{8,9},{9,8},{10,11... | collective-permute-start | bytes 1572872 | tf_op jit(solution)/shard_map/ppermute | solution.py:229
  232.9 30.5 %copy-start.2 = (f32[16,128]{1,0:T(8,128)}, f32[16,128]{1,0:T(8,128)S(1)}, u32[]{:S(2)}) copy-start(f32[16,128]{1,0:T(8,128)S(1)} %reduce_sum.9.own_ref) | copy-start | bytes 24580
  256.1 7.3 %copy-start = (f32[64,16,128]{2,1,0:T(8,128)}, f32[64,16,128]{2,1,0:T(8,128)S(1)}, u32[]{:S(2)}) copy-start(f32[64,16,128]{2,1,0:T(8,128)S(1)} %all_to_all.16.mine_ref) | copy-start | bytes 1572868
  256.1 7.3 %collective-permute-start.1 = (f32[64,16,128]{2,1,0:T(8,128)S(1)}, f32[64,16,128]{2,1,0:T(8,128)S(1)}, u32[]{:S(2)}, u32[]{:S(2)}) collective-permute-start(f32[64,16,128]{2,1,0:T(8,128)S(1)} %all_to_all.16.mine_ref), channel_id=1, source_target_pairs={{0,1},{1,0},{2,3},{3,2},{4,5},{5,4},{6,7},{7,6},{8,9},{9,8},{10,11... | collective-permute-start | bytes 1572872 | tf_op jit(solution)/shard_map/ppermute | solution.py:234
  263.4 0.8 copy-start.1

commit v3 on v2

--- a/solution.py
+++ b/solution.py
@@ -31,71 +31,58 @@
     return jnp.where(flag, 1.0, 0.0).astype(BF)
 
 
-def pack_kernel(main_steps, spare, ids_ref, rows_ref, basis_ref, out_ref, normed_ref, rank_ref, pick_ref, fan_ref):
-    step = pl.program_id(0)
+def pack_kernel(main_steps, spare, ids_ref, rows_ref, basis_ref, out_ref, buf, fan, sems):
     tops, row_count = ids_ref.shape
     experts = out_ref.shape[0]
-
-    @pl.when(step == 0)
-    def _():
-        values = rows_ref[...].astype(F32)
-        power = jnp.mean(values * values, axis=1, keepdims=True) + epsilon
-        normed = (values / jnp.sqrt(power)).astype(BF)
+    steps = main_steps + spare + 1
+    copies = [
+        pltpu.make_async_copy(buf.at[i], out_ref.at[:, pl.ds(STEP * i, STEP), :], sems.at[i]) for i in range(steps)
+    ]
+    buf[steps - 1] = jnp.broadcast_to(basis_ref[...].astype(BF)[None], (experts, STEP, LANES))
+    copies[steps - 1].start()
+    values = rows_ref[...].astype(F32)
+    power = jnp.mean(values * values, axis=1, keepdims=True) + epsilon
+    normed = (values / jnp.sqrt(power)).astype(BF)
+    member = jnp.zeros((experts, row_count), F32)
+    for top in range(tops):
+        named = jnp.broadcast_to(ids_ref[top:top + 1, :], (experts, row_count))
+        member = member + jnp.where(named == iota((experts, row_count), 0), 1.0, 0.0)
+    ahead = as_bf16(iota((row_count, row_count), 0) <= iota((row_count, row_count), 1))
+    rank = jnp.where(member > 0.0, dot(member.astype(BF), ahead), 0.0)
+    slots = experts * MAIN
+    owner = as_bf16(iota((slots, experts), 0) // MAIN == iota((slots, experts), 1))
+    wanted = (iota((slots, row_count), 0) % MAIN + 1).astype(F32)
+    pick = as_bf16(dot(owner, rank.astype(BF)) == wanted)
+    for t in range(main_steps):
+        both = dot(pick, normed[:, 2 * LANES * t:2 * LANES * (t + 1)]).astype(BF)
+        buf[t, :, 0:MAIN, :] = both[:, :LANES].reshape(experts, MAIN, LANES)
+        buf[t, :, MAIN:, :] = both[:, LANES:].reshape(experts, MAIN, LANES)
+        copies[t].start()
+    for k in range(spare):
+        late = as_bf16(rank == MAIN + k + 1.0)
         for t in range(main_steps):
-            normed_ref[t] = normed[:, 2 * LANES * t:2 * LANES * (t + 1)]
-        member = jnp.zeros((experts, row_count), F32)
-        for top in range(tops):
-            named = jnp.broadcast_to(ids_ref[top:top + 1, :], (experts, row_count))
-            member = member + jnp.where(named == iota((experts, row_count), 0), 1.0, 0.0)
-        ahead = as_bf16(iota((row_count, row_count), 0) <= iota((row_count, row_count), 1))
-        rank = jnp.where(member > 0.0, dot(member.astype(BF), ahead), 0.0)
-        rank_ref[...] = rank
-        slots = experts * MAIN
-        owner = as_bf16(iota((slots, experts), 0) // MAIN == iota((slots, experts), 1))
-        wanted = (iota((slots, row_count), 0) % MAIN + 1).astype(F32)
-        pick_ref[...] = as_bf16(dot(owner, rank.astype(BF)) == wanted)
-
-    @pl.when(step < main_steps)
-    def _():
-        both = dot(pick_ref[...], normed_ref[step]).astype(BF)
-        out_ref[:, 0:MAIN, :] = both[:, :LANES].reshape(experts, MAIN, LANES)
-        out_ref[:, MAIN:, :] = both[:, LANES:].reshape(experts, MAIN, LANES)
-
-    @pl.when((step >= main_steps) & (step < main_steps + spare))
-    def _():
-        wanted = (step - main_steps + MAIN + 1).astype(F32)
-        pick = as_bf16(rank_ref[...] == wanted)
-        for t in range(main_steps):
-            both = dot(pick, normed_ref[t])
-            fan_ref[pl.ds(2 * t, experts, stride=STEP), :] = both[:, :LANES]
-            fan_ref[pl.ds(2 * t + 1, experts, stride=STEP), :] = both[:, LANES:]
-        out_ref[...] = fan_ref[...].reshape(experts, STEP, LANES).astype(BF)
-
-    @pl.when(step == main_steps + spare)
-    def _():
-        basis = basis_ref[...].astype(BF)
-        out_ref[...] = jnp.broadcast_to(basis[None], out_ref.shape)
+            both = dot(late, normed[:, 2 * LANES * t:2 * LANES * (t + 1)])
+            fan[k, pl.ds(2 * t, experts, stride=STEP), :] = both[:, :LANES]
+            fan[k, pl.ds(2 * t + 1, experts, stride=STEP), :] = both[:, LANES:]
+        buf[main_steps + k] = fan[k].reshape(experts, STEP, LANES).astype(BF)
+        copies[main_steps + k].start()
+    for copy in copies:
+        copy.wait()
 
 
 def pack(ids_t, rows, basis, experts, spare):
-    row_count, width = rows.shape
-    main_steps = width // (2 * LANES)
-    steps = main_steps + spare + 1
+    main_steps = rows.shape[1] // (2 * LANES)
+    steps = main_steps + spare + 1
+    vmem = pl.BlockSpec(memory_space=pltpu.VMEM)
     return pl.pallas_call(
         lambda *refs: pack_kernel(main_steps, spare, *refs),
-        grid=(steps,),
         out_shape=jax.ShapeDtypeStruct((experts, STEP * steps, LANES), BF),
-        in_specs=[
-            pl.BlockSpec(ids_t.shape, lambda i: (0, 0)),
-            pl.BlockSpec(rows.shape, lambda i: (0, 0)),
-            pl.BlockSpec(basis.shape, lambda i: (0, 0)),
-        ],
-        out_specs=pl.BlockSpec((experts, STEP, LANES), lambda i: (0, i, 0)),
+        in_specs=[vmem, vmem, vmem],
+        out_specs=pl.BlockSpec(memory_space=pl.ANY),
         scratch_shapes=[
-            pltpu.VMEM((main_steps, row_count, 2 * LANES), BF),
-            pltpu.VMEM((experts, row_count), F32),
-            pltpu.VMEM((experts * MAIN, row_count), BF),
-            pltpu.VMEM((experts * STEP, LANES), F32),
+            pltpu.VMEM((steps, experts, STEP, LANES), BF),
+            pltpu.VMEM((spare, experts * STEP, LANES), F32),
+            pltpu.SemaphoreType.DMA((steps,)),
         ],
         name="pack",
     )(ids_t, rows, basis)
@@ -129,16 +116,15 @@
         at = 2 * LANES * t
         x[0:main, at:at + LANES] = buf[t, :, 0:MAIN, :].reshape(main, LANES)
         x[0:main, at + LANES:at + 2 * LANES] = buf[t, :, MAIN:, :].reshape(main, LANES)
-        part = dot(x[:, at:at + 2 * LANES], basis[at:at + 2 * LANES, :])
-        first = part if first is None else first + part
     rows = x[...]
-    second = dot(first.astype(BF), rows, ((0,), (0,))).astype(BF)
+    first = dot(basis, rows, ((0,), (1,)))
+    second = dot(first.astype(BF), rows).astype(BF)
     load_w.wait()
     weight = w[...]
     inner = dot(second, weight, ((1,), (1,))).astype(BF)
     back = dot(inner, weight).astype(BF)
-    again = dot(rows, back, ((1,), (1,))).astype(BF)
-    term = dot(again, rows, ((0,), (0,)))
+    again = dot(back, rows, ((1,), (1,))).astype(BF)
+    term = dot(again, rows)
     y[...] = term.T.reshape(y.shape)
     keep_ref[...] = y[:, core]
     send_ref[...] = y[:, 1 - core]
@@ -174,11 +160,10 @@
     core = core_ref[0]
     load_w = pltpu.make_async_copy(weight_ref, w, w_sem)
     load_w.start()
-    z[:, core] = mine_ref[...]
-    z[:, 1 - core] = other_ref[...]
-    size = z.shape[0] * z.shape[1] * z.shape[2]
-    total = z[...].reshape(size, LANES)
-    raw = dot(total, total, ((0,), (0,)), HI)
+    size = z.shape[0] * STEP
+    mine = mine_ref[...].reshape(size, LANES)
+    other = other_ref[...].reshape(size, LANES)
+    raw = dot(mine, mine, ((0,), (0,)), HI) + dot(other, other, ((0,), (0,)), HI)
     diagonal = iota((LANES, LANES), 0) == iota((LANES, LANES), 1)
     eye = jnp.where(diagonal, 1.0, 0.0)
     power = jnp.sum(jnp.where(diagonal, raw, 0.0), keepdims=True) + epsilon
@@ -190,10 +175,12 @@
         product = factor if product is None else dot(product, factor, precision=HI)
         if step + 1 < NS_STEPS:
             gram = dot(dot(factor, gram, precision=HI), factor, precision=HI)
-    whole = dot(total * scale, product, precision=HI)
-    local_ref[...] = dot(own_ref[...] * scale, product, precision=HI)
+    final = product * scale
+    z[:, core] = dot(mine, final, precision=HI).astype(BF).reshape(mine_ref.shape)
+    z[:, 1 - core] = dot(other, final, precision=HI).astype(BF).reshape(mine_ref.shape)
+    local_ref[...] = dot(own_ref[...], final, precision=HI)
     load_w.wait()
-    packed_ref[...] = dot(w[...], whole.astype(BF)).astype(BF)
+    packed_ref[...] = dot(w[...], z[...].reshape(2 * size, LANES)).astype(BF)
 
 
 def ortho(core, mine, other, own, weight):
@@ -207,7 +194,7 @@
         in_specs=[pl.BlockSpec(memory_space=pltpu.SMEM), vmem, vmem, vmem, pl.BlockSpec(memory_space=pl.ANY)],
         out_specs=(vmem, vmem),
         scratch_shapes=[
-            pltpu.VMEM((mine.shape[0], 2) + mine.shape[1:], F32),
+            pltpu.VMEM((mine.shape[0], 2) + mine.shape[1:], BF),
             pltpu.VMEM(weight.shape, BF),
             pltpu.SemaphoreType.DMA,
         ],

time: 273 us -> 264 us (0.967)
  Pallas kernels: 31.4 us -> 22.8 us
    pallas_call x1, Pallas kernels: 8.36 us -> 4.64 us  [pack(): pl.pallas_call(lambda *refs: pack_kernel(main_steps, spare, *refs), out_s...]
    pallas_call x1, Pallas kernels: 14.8 us -> 11.3 us  [chain(): pl.pallas_call(lambda *refs: chain_kernel(main_steps, spare, *refs), out_...]
where the time goes in v3:
time: 264 us
  waiting for transfers between devices  146 us (55%)
  blocking collectives  64.5 us (24%)
  starting transfers between devices  27.8 us (11%)
  Pallas kernels  22.8 us (9%)
    all_to_all x1, waiting for transfers between devices, shards(): lax.all_to_all(sent, ('chip', 'core'), split_axis=0, concat_axis=0, tiled...  143 us
    all_to_all x1, blocking collectives, shards(): lax.all_to_all(half, 'chip', split_axis=0, concat_axis=0, tiled=True)  41.4 us
    all_to_all x1, blocking collectives, shards(): lax.all_to_all(spread, 'chip', split_axis=0, concat_axis=0, tiled=True)  23.1 us
    all_to_all x1, starting transfers between devices, shards(): lax.all_to_all(sent, ('chip', 'core'), split_axis=0, concat_axis=0, tiled...  18.8 us
    pallas_call x1, Pallas kernels, chain(): pl.pallas_call(lambda *refs: chain_kernel(main_steps, spare, *refs), out_...  11.3 us
    pallas_call x1, Pallas kernels, ortho(): pl.pallas_call(ortho_kernel, out_shape=(jax.ShapeDtypeStruct((weight.shap...  6.85 us
    ppermute x1, starting transfers between devices, shards(): other = lax.ppermute(mine, 'core', swap)  5.81 us
  transfers between devices with their start and end apart: 3, of which 3 were waited for; matrix products, arithmetic and copies ran while one was open for 0% of the time, Pallas kernels for 0%

profile of v3, /device:TPU:1, one launch (start us, length us, event | category | flops | bytes accessed | tf_op | source)
XLA Modules:
  0.0 264.0 jit_solution(2620324018145002199)
XLA Ops:
  0.6 4.6 %pack.1 = bf16[128,176,128]{2,1,0:T(8,128)(2,1)} custom-call(s32[8,128]{1,0:T(8,128)} %bitcast.6, bf16[128,2048]{1,0:T(8,128)(2,1)} %refs_1_.1, f32[16,128]{1,0:T(8,128)} %refs_2_.1), custom_call_target="tpu_custom_call" | custom-call | tf_op jit(solution)/shard_map/pack/pallas_call | solution.py:77
  5.3 18.8 %all-to-all-start = ((bf16[128,176,128]{2,1,0:T(8,128)(2,1)}), bf16[128,176,128]{2,1,0:T(8,128)(2,1)}, u32[]{:S(2)}, u32[]{:S(2)}) async-start(bf16[128,176,128]{2,1,0:T(8,128)(2,1)} %pack.1), calls=%async_computation | async-start | bytes 11534336 | tf_op jit(solution)/shard_map/all_to_all | solution.py:214
  24.1 142.8 %all-to-all-done.refs_1_ = bf16[128,176,128]{2,1,0:T(8,128)(2,1)} async-done(((bf16[128,176,128]{2,1,0:T(8,128)(2,1)}), bf16[128,176,128]{2,1,0:T(8,128)(2,1)}, u32[]{:S(2)}, u32[]{:S(2)}) %all-to-all-start) | async-done | bytes 5767200 | tf_op jit(solution)/shard_map/all_to_all | solution.py:214
  166.9 11.3 %chain.1 = (f32[64,16,128]{2,1,0:T(8,128)}, f32[64,16,128]{2,1,0:T(8,128)}) custom-call(s32[1]{0:T(128)} %bitcast.refs_0_.core_ref, bf16[128,176,128]{2,1,0:T(8,128)(2,1)} %all-to-all-done.refs_1_, bf16[768,2048]{1,0:T(8,128)(2,1)} %bitcast.4), custom_call_target="tpu_custom_call" | custom-call | tf_op jit(solution)/shard_map/chain/pallas_call | solution.py:141
  178.2 3.2 %collective-permute-start = (f32[64,16,128]{2,1,0:T(8,128)}, f32[64,16,128]{2,1,0:T(8,128)S(1)}, u32[]{:S(2)}, u32[]{:S(2)}) collective-permute-start(f32[64,16,128]{2,1,0:T(8,128)} %get-tuple-element.7), channel_id=1, source_target_pairs={{0,1},{1,0},{2,3},{3,2},{4,5},{5,4},{6,7},{7,6},{8,9},{9,8},{10,11... | collective-permute-start | bytes 1572872 | tf_op jit(solution)/shard_map/ppermute | solution.py:216
  181.4 1.7 collective-permute-done
  183.1 1.1 add.3
  184.2 41.4 %all_to_all.15 = f32[64,16,128]{2,1,0:T(8,128)S(1)} all-to-all(f32[64,16,128]{2,1,0:T(8,128)S(1)} %add.3), channel_id=1, replica_groups=mesh['layer'=4,'chip'=64,'core'=2] {'chip'}, dimensions={0} | all-to-all | bytes 1048576 | tf_op jit(solution)/shard_map/all_to_all | solution.py:217
  225.6 0.1 reduce_sum.9.own_ref
  225.7 0.0 copy-start.2
  225.8 23.1 %all_to_all.16.mine_ref = f32[64,16,128]{2,1,0:T(8,128)S(1)} all-to-all(f32[64,16,128]{2,1,0:T(8,128)S(1)} %broadcast_in_dim.4), channel_id=1, replica_groups=mesh['layer'=4,'chip'=64,'core'=2] {'chip'}, dimensions={0} | all-to-all | bytes 1048576 | tf_op jit(solution)/shard_map/all_to_all | solution.py:220
  248.8 0.0 copy-start
  248.8 5.8 %collective-permute-start.1 = (f32[64,16,128]{2,1,0:T(8,128)S(1)}, f32[64,16,128]{2,1,0:T(8,128)S(1)}, u32[]{:S(2)}, u32[]{:S(2)}) collective-permute-start(f32[64,16,128]{2,1,0:T(8,128)S(1)} %all_to_all.16.mine_ref), channel_id=1, source_target_pairs={{0,1},{1,0},{2,3},{3,2},{4,5},{5,4},{6,7},{7,6},{8,9},{9,8},{10,11... | collective-permute-start | bytes 1572872 | tf_op jit(solution)/shard_map/ppermute | solution.py:221
  254.7 1.5 collective-permute-done.1.other_ref
  256.2 0.0 copy-done.2
  256.2 0.0 copy-done
  256.2 0.0 copy-start.1
  256.2 0.8 copy-done.1
  257.0 6.8 %ortho.1 = (bf16[768,128]{1,0:T(8,128)(2,1)}, f32[16,128]{1,0:T(8,128)}) custom-call(s32[1]{0:T(128)} %bitcast.refs_0_.core_ref, f32[64,16,128]{2,1,0:T(8,128)} %copy-done, f32[64,16,128]{2,1,0:T(8,128)} %copy-done.1, f32[16,128]{1,0:T(8,128)} %copy-done.2, bf16[768,2048]{1,0:T(8,128)(2,1)} %bitcast.5), custom_call_target="tpu_custom_call" | custom-call | tf_op jit(solution)/shard_map/ortho/pallas_call | solution.py:188
  (1 shorter events, 0.0 us)
Async XLA Ops:
  5.3 161.6 %all-to-all-start = ((bf16[128,176,128]{2,1,0:T(8,128)(2,1)}), bf16[128,176,128]{2,1,0:T(8,128)(2,1)}, u32[]{:S(2)}, u32[]{:S(2)}) async-start(bf16[128,176,128]{2,1,0:T(8,128)(2,1)} %pack.1), calls=%async_computation | async-start | bytes 11534336 | tf_op jit(solution)/shard_map/all_to_all | solution.py:214
  178.2 4.9 %collective-permute-start = (f32[64,16,128]{2,1,0:T(8,128)}, f32[64,16,128]{2,1,0:T(8,128)S(1)}, u32[]{:S(2)}, u32[]{:S(2)}) collective-permute-start(f32[64,16,128]{2,1,0:T(8,128)} %get-tuple-element.7), channel_id=1, source_target_pairs={{0,1},{1,0},{2,3},{3,2},{4,5},{5,4},{6,7},{7,6},{8,9},{9,8},{10,11... | collective-permute-start | bytes 1572872 | tf_op jit(solution)/shard_map/ppermute | solution.py:216
  225.7 30.5 %copy-start.2 = (f32[16,128]{1,0:T(8,128)}, f32[16,128]{1,0:T(8,128)S(1)}, u32[]{:S(2)}) copy-start(f32[16,128]{1,0:T(8,128)S(1)} %reduce_sum.9.own_ref) | copy-start | bytes 24580
  248.8 7.3 %copy-start = (f32[64,16,128]{2,1,0:T(8,128)}, f32[64,16,128]{2,1,0:T(8,128)S(1)}, u32[]{:S(2)}) copy-start(f32[64,16,128]{2,1,0:T(8,128)S(1)} %all_to_all.16.mine_ref) | copy-start | bytes 1572868
  248.8 7.3 %collective-permute-start.1 = (f32[64,16,128]{2,1,0:T(8,128)S(1)}, f32[64,16,128]{2,1,0:T(8,128)S(1)}, u32[]{:S(2)}, u32[]{:S(2)}) collective-permute-start(f32[64,16,128]{2,1,0:T(8,128)S(1)} %all_to_all.16.mine_ref), channel_id=1, source_target_pairs={{0,1},{1,0},{2,3},{3,2},{4,5},{5,4},{6,7},{7,6},{8,9},{9,8},{10,11... | collective-permute-start | bytes 1572872 | tf_op jit(solution)/shard_map/ppermute | solution.py:221
  256.2 0.8 copy-start.1

commit v4 on v3

--- a/solution.py
+++ b/solution.py
@@ -31,69 +31,73 @@
     return jnp.where(flag, 1.0, 0.0).astype(BF)
 
 
-def pack_kernel(main_steps, spare, ids_ref, rows_ref, basis_ref, out_ref, buf, fan, sems):
+def pack_kernel(main_steps, spare, side_ref, ids_ref, rows_ref, basis_ref, *rest):
+    out_ref, buf, fan, sems = rest[-4:]
+    core, slot = side_ref[0], side_ref[1]
     tops, row_count = ids_ref.shape
-    experts = out_ref.shape[0]
-    steps = main_steps + spare + 1
-    copies = [
-        pltpu.make_async_copy(buf.at[i], out_ref.at[:, pl.ds(STEP * i, STEP), :], sems.at[i]) for i in range(steps)
-    ]
-    buf[steps - 1] = jnp.broadcast_to(basis_ref[...].astype(BF)[None], (experts, STEP, LANES))
+    chips = out_ref.shape[0]
+    steps = main_steps + spare + 1
+    copies = [pltpu.make_async_copy(buf.at[i], out_ref.at[:, 2 * i + slot], sems.at[i]) for i in range(steps)]
+    buf[steps - 1] = jnp.broadcast_to(basis_ref[...][None], (chips, STEP, LANES))
     copies[steps - 1].start()
     values = rows_ref[...].astype(F32)
     power = jnp.mean(values * values, axis=1, keepdims=True) + epsilon
     normed = (values / jnp.sqrt(power)).astype(BF)
-    member = jnp.zeros((experts, row_count), F32)
+    owner_names = (2 * iota((chips, row_count), 0) + core).astype(F32)
+    member = jnp.zeros((chips, row_count), F32)
     for top in range(tops):
-        named = jnp.broadcast_to(ids_ref[top:top + 1, :], (experts, row_count))
-        member = member + jnp.where(named == iota((experts, row_count), 0), 1.0, 0.0)
+        named = jnp.broadcast_to(ids_ref[top:top + 1, :].astype(F32), (chips, row_count))
+        member = member + jnp.where(named == owner_names, 1.0, 0.0)
     ahead = as_bf16(iota((row_count, row_count), 0) <= iota((row_count, row_count), 1))
     rank = jnp.where(member > 0.0, dot(member.astype(BF), ahead), 0.0)
-    slots = experts * MAIN
-    owner = as_bf16(iota((slots, experts), 0) // MAIN == iota((slots, experts), 1))
+    slots = chips * MAIN
+    owner = as_bf16(iota((slots, chips), 0) // MAIN == iota((slots, chips), 1))
     wanted = (iota((slots, row_count), 0) % MAIN + 1).astype(F32)
     pick = as_bf16(dot(owner, rank.astype(BF)) == wanted)
     for t in range(main_steps):
         both = dot(pick, normed[:, 2 * LANES * t:2 * LANES * (t + 1)]).astype(BF)
-        buf[t, :, 0:MAIN, :] = both[:, :LANES].reshape(experts, MAIN, LANES)
-        buf[t, :, MAIN:, :] = both[:, LANES:].reshape(experts, MAIN, LANES)
+        buf[t, :, 0:MAIN, :] = both[:, :LANES].reshape(chips, MAIN, LANES)
+        buf[t, :, MAIN:, :] = both[:, LANES:].reshape(chips, MAIN, LANES)
         copies[t].start()
     for k in range(spare):
         late = as_bf16(rank == MAIN + k + 1.0)
         for t in range(main_steps):
             both = dot(late, normed[:, 2 * LANES * t:2 * LANES * (t + 1)])
-            fan[k, pl.ds(2 * t, experts, stride=STEP), :] = both[:, :LANES]
-            fan[k, pl.ds(2 * t + 1, experts, stride=STEP), :] = both[:, LANES:]
-        buf[main_steps + k] = fan[k].reshape(experts, STEP, LANES).astype(BF)
+            fan[k, pl.ds(2 * t, chips, stride=STEP), :] = both[:, :LANES]
+            fan[k, pl.ds(2 * t + 1, chips, stride=STEP), :] = both[:, LANES:]
+        buf[main_steps + k] = fan[k].reshape(chips, STEP, LANES).astype(BF)
         copies[main_steps + k].start()
     for copy in copies:
         copy.wait()
 
 
-def pack(ids_t, rows, basis, experts, spare):
+def pack(side, ids, rows, basis, filled, chips, spare):
     main_steps = rows.shape[1] // (2 * LANES)
     steps = main_steps + spare + 1
     vmem = pl.BlockSpec(memory_space=pltpu.VMEM)
+    hbm = pl.BlockSpec(memory_space=pl.ANY)
     return pl.pallas_call(
         lambda *refs: pack_kernel(main_steps, spare, *refs),
-        out_shape=jax.ShapeDtypeStruct((experts, STEP * steps, LANES), BF),
-        in_specs=[vmem, vmem, vmem],
-        out_specs=pl.BlockSpec(memory_space=pl.ANY),
+        out_shape=jax.ShapeDtypeStruct((chips, 2 * steps, STEP, LANES), BF),
+        in_specs=[pl.BlockSpec(memory_space=pltpu.SMEM), vmem, vmem, vmem] + [hbm] * len(filled),
+        out_specs=hbm,
         scratch_shapes=[
-            pltpu.VMEM((steps, experts, STEP, LANES), BF),
-            pltpu.VMEM((spare, experts * STEP, LANES), F32),
+            pltpu.VMEM((steps, chips, STEP, LANES), BF),
+            pltpu.VMEM((spare, chips * STEP, LANES), F32),
             pltpu.SemaphoreType.DMA((steps,)),
         ],
+        input_output_aliases={4: 0} if filled else {},
+        cost_estimate=pl.CostEstimate(flops=400_000_000, bytes_accessed=4_000_000, transcendentals=0),
         name="pack",
-    )(ids_t, rows, basis)
+    )(side, ids, rows, basis, *filled)
 
 
 def chain_kernel(main_steps, spare, core_ref, got_ref, weight_ref, keep_ref, send_ref, buf, x, w, fan, y, sems, w_sem):
     steps = main_steps + spare + 1
-    group = got_ref.shape[0]
+    group = 2 * got_ref.shape[0]
     core = core_ref[0]
     copies = [
-        pltpu.make_async_copy(got_ref.at[:, pl.ds(STEP * i, STEP), :], buf.at[i], sems.at[i]) for i in range(steps)
+        pltpu.make_async_copy(got_ref.at[:, pl.ds(2 * i, 2)], buf.at[i], sems.at[i]) for i in range(steps)
     ]
     load_w = pltpu.make_async_copy(weight_ref, w, w_sem)
     order = [steps - 1] + list(range(main_steps, main_steps + spare)) + list(range(main_steps))
@@ -114,8 +118,8 @@
     for t in range(main_steps):
         copies[t].wait()
         at = 2 * LANES * t
-        x[0:main, at:at + LANES] = buf[t, :, 0:MAIN, :].reshape(main, LANES)
-        x[0:main, at + LANES:at + 2 * LANES] = buf[t, :, MAIN:, :].reshape(main, LANES)
+        x[0:main, at:at + LANES] = buf[t, :, :, 0:MAIN, :].reshape(main, LANES)
+        x[0:main, at + LANES:at + 2 * LANES] = buf[t, :, :, MAIN:, :].reshape(main, LANES)
     rows = x[...]
     first = dot(basis, rows, ((0,), (1,)))
     second = dot(first.astype(BF), rows).astype(BF)
@@ -131,7 +135,7 @@
 
 
 def chain(core, got, weight, spare):
-    group = got.shape[0]
+    group = 2 * got.shape[0]
     width = weight.shape[1]
     main_steps = width // (2 * LANES)
     steps = main_steps + spare + 1
@@ -144,7 +148,7 @@
         in_specs=[pl.BlockSpec(memory_space=pltpu.SMEM), hbm, hbm],
         out_specs=(vmem, vmem),
         scratch_shapes=[
-            pltpu.VMEM((steps, group, STEP, LANES), BF),
+            pltpu.VMEM((steps, group // 2, 2, STEP, LANES), BF),
             pltpu.VMEM((group * (MAIN + spare), width), BF),
             pltpu.VMEM(weight.shape, BF),
             pltpu.VMEM((group * STEP, LANES), F32),
@@ -208,10 +212,18 @@
     capacity = max(2, min(row_count, row_count * expert_ids.shape[1] * 5 // (4 * experts)))
     spare = capacity - MAIN
     weight = weights[0]
+    chips = experts // 2
     core = lax.axis_index("core").astype(jnp.int32).reshape(1)
     swap = [(0, 1), (1, 0)]
-    sent = pack(expert_ids.T, rows, start_basis, experts, spare)
-    got = lax.all_to_all(sent, ("chip", "core"), split_axis=0, concat_axis=0, tiled=True)
+    tops = expert_ids.shape[1]
+    small = jnp.concatenate([expert_ids.T.astype(BF), start_basis.astype(BF)], axis=0)
+    rows_there = lax.ppermute(rows, "core", swap)
+    small_there = lax.ppermute(small, "core", swap)
+    here = jnp.concatenate([core, core])
+    there = jnp.concatenate([core, 1 - core])
+    sent = pack(here, small[:tops], rows, small[tops:], (), chips, spare)
+    sent = pack(there, small_there[:tops], rows_there, small_there[tops:], (sent,), chips, spare)
+    got = lax.all_to_all(sent, "chip", split_axis=0, concat_axis=0, tiled=True)
     keep, send = chain(core, got, weight, spare)
     half = keep + lax.ppermute(send, "core", swap)
     parts = lax.all_to_all(half, "chip", split_axis=0, concat_axis=0, tiled=True)

time: 264 us -> 252 us (0.955)
  waiting for transfers between devices: 146 us -> 3.25 us
  blocking collectives: 64.5 us -> 194 us
  starting transfers between devices: 27.8 us -> 22.6 us
    all_to_all x1 -> x0, waiting for transfers between devices: 143 us -> none  [shards(): lax.all_to_all(sent, ('chip', 'core'), split_axis=0, concat_axis=0, tiled...]
    all_to_all x0 -> x1, blocking collectives: none -> 139 us  [shards(): got = lax.all_to_all(sent, 'chip', split_axis=0, concat_axis=0, tiled=True)]
    all_to_all x1 -> x0, starting transfers between devices: 18.8 us -> none  [shards(): lax.all_to_all(sent, ('chip', 'core'), split_axis=0, concat_axis=0, tiled...]
    ppermute x0 -> x2, starting transfers between devices: none -> 10.7 us  [the longest x1 8.75 us: shards(): rows_there = lax.ppermute(rows, 'core', swap)]
    all_to_all x1, blocking collectives: 41.4 us -> 31.7 us  [shards(): lax.all_to_all(half, 'chip', split_axis=0, concat_axis=0, tiled=True)]
    ppermute x1, starting transfers between devices: 3.17 us -> 6.14 us  [shards(): half = keep + lax.ppermute(send, 'core', swap)]
    pallas_call x1 -> x2, Pallas kernels: 4.64 us -> 6.79 us  [pack(): pl.pallas_call(lambda *refs: pack_kernel(main_steps, spare, *refs), out_s...]
  transfers between devices with their start and end apart: 3 -> 4, of which waited for: 3 -> 2; matrix products, arithmetic and copies ran while one was open for 0% -> 1% of each run, Pallas kernels for 0% -> 1%
where the time goes in v4:
time: 252 us
  blocking collectives  194 us (77%)
  Pallas kernels  24.9 us (10%)
  starting transfers between devices  22.6 us (9%)
  waiting for transfers between devices  3.25 us (1%)
  other arithmetic  3.19 us (1%)
  local copies, waits for them, and re-layouts  2.8 us (1%)
    all_to_all x1, blocking collectives, shards(): got = lax.all_to_all(sent, 'chip', split_axis=0, concat_axis=0, tiled=True)  139 us
    all_to_all x1, blocking collectives, shards(): lax.all_to_all(half, 'chip', split_axis=0, concat_axis=0, tiled=True)  31.7 us
    all_to_all x1, blocking collectives, shards(): lax.all_to_all(spread, 'chip', split_axis=0, concat_axis=0, tiled=True)  23.1 us
    pallas_call x1, Pallas kernels, chain(): pl.pallas_call(lambda *refs: chain_kernel(main_steps, spare, *refs), out_...  11.3 us
    ppermute x1, starting transfers between devices, shards(): rows_there = lax.ppermute(rows, 'core', swap)  8.75 us
    pallas_call x1, Pallas kernels, ortho(): pl.pallas_call(ortho_kernel, out_shape=(jax.ShapeDtypeStruct((weight.shap...  6.85 us
    pallas_call x2, Pallas kernels, pack(): pl.pallas_call(lambda *refs: pack_kernel(main_steps, spare, *refs), out_s...  6.79 us
    ppermute x1, starting transfers between devices, shards(): half = keep + lax.ppermute(send, 'core', swap)  6.14 us
  transfers between devices with their start and end apart: 4, of which 2 were waited for; matrix products, arithmetic and copies ran while one was open for 1% of the time, Pallas kernels for 1%

profile of v4, /device:TPU:1, one launch (start us, length us, event | category | flops | bytes accessed | tf_op | source)
XLA Modules:
  0.0 251.9 jit_solution(18028424873095624044)
XLA Ops:
  0.6 8.7 %collective-permute-start.1 = (bf16[128,2048]{1,0:T(8,128)(2,1)}, bf16[128,2048]{1,0:T(8,128)(2,1)S(1)}, u32[]{:S(2)}, u32[]{:S(2)}) collective-permute-start(bf16[128,2048]{1,0:T(8,128)(2,1)} %refs_2_.1), channel_id=1, source_target_pairs={{0,1},{1,0},{2,3},{3,2},{4,5},{5,4},{6,7},{7,6},{8,9},{9,8},{10,11... | collective-permute-start | bytes 1572872 | tf_op jit(solution)/shard_map/ppermute | solution.py:220
  9.4 0.7 convert_element_type.10.refs_3_
  10.1 0.0 copy-start.4
  10.1 0.7 convert_bitcast_fusion.refs_1_
  10.8 0.0 copy-start.5
  10.8 1.9 collective-permute-start
  12.7 0.6 pad_add_fusion
  13.3 0.0 copy-done.4
  13.3 0.0 copy-done.5
  13.3 3.4 %pack.2.refs_4_ = bf16[64,22,16,128]{3,2,1,0:T(8,128)(2,1)} custom-call(s32[2]{0:T(128)} %get-tuple-element.11.refs_0_, bf16[8,128]{1,0:T(8,128)(2,1)} %copy-done.5, bf16[128,2048]{1,0:T(8,128)(2,1)} %refs_2_.1, bf16[16,128]{1,0:T(8,128)(2,1)} %copy-done.4), custom_call_target="tpu_custom_call" | custom-call | flops 400000000 | bytes 4000000 | tf_op jit(solution)/shard_map/pack/pallas_call | solution.py:79
  16.7 0.0 collective-permute-done
  16.7 0.6 slice.8.refs_1_
  17.3 0.6 slice.9.refs_3_
  17.9 0.0 collective-permute-done.1.refs_2_
  17.9 0.0 copy-start.1
  17.9 0.8 copy-done.1
  18.7 3.4 %pack.3 = bf16[64,22,16,128]{3,2,1,0:T(8,128)(2,1)} custom-call(s32[2]{0:T(128)} %get-tuple-element.10.refs_0_, bf16[8,128]{1,0:T(8,128)(2,1)} %slice.8.refs_1_, bf16[128,2048]{1,0:T(8,128)(2,1)} %copy-done.1, bf16[16,128]{1,0:T(8,128)(2,1)} %slice.9.refs_3_, bf16[64,22,16,128]{3,2,1,0:T(8,128)(2,1)} %pack.2.refs_4_), custom_call_target="tpu_custom_call", output_to_operand_aliasing={{}: (4, {})} | custom-call | flops 400000000 | bytes 4000000 | tf_op jit(solution)/shard_map/pack/pallas_call | solution.py:79
  22.1 139.5 %all_to_all.15.refs_1_ = bf16[64,22,16,128]{3,2,1,0:T(8,128)(2,1)} all-to-all(bf16[64,22,16,128]{3,2,1,0:T(8,128)(2,1)} %pack.3), channel_id=1, replica_groups=mesh['layer'=4,'chip'=64,'core'=2] {'chip'}, dimensions={0} | all-to-all | bytes 11534336 | tf_op jit(solution)/shard_map/all_to_all | solution.py:226
  161.6 11.3 %chain.1 = (f32[64,16,128]{2,1,0:T(8,128)}, f32[64,16,128]{2,1,0:T(8,128)}) custom-call(s32[1]{0:T(128)} %bitcast.refs_0_.core_ref, bf16[64,22,16,128]{3,2,1,0:T(8,128)(2,1)} %all_to_all.15.refs_1_, bf16[768,2048]{1,0:T(8,128)(2,1)} %bitcast.5), custom_call_target="tpu_custom_call" | custom-call | tf_op jit(solution)/shard_map/chain/pallas_call | solution.py:145
  172.8 6.1 %collective-permute-start.2 = (f32[64,16,128]{2,1,0:T(8,128)}, f32[64,16,128]{2,1,0:T(8,128)S(1)}, u32[]{:S(2)}, u32[]{:S(2)}) collective-permute-start(f32[64,16,128]{2,1,0:T(8,128)} %get-tuple-element.7), channel_id=1, source_target_pairs={{0,1},{1,0},{2,3},{3,2},{4,5},{5,4},{6,7},{7,6},{8,9},{9,8},{10,11... | collective-permute-start | bytes 1572872 | tf_op jit(solution)/shard_map/ppermute | solution.py:228
  179.0 1.7 collective-permute-done.2
  180.7 1.1 add.3
  181.8 31.7 %all_to_all.16 = f32[64,16,128]{2,1,0:T(8,128)S(1)} all-to-all(f32[64,16,128]{2,1,0:T(8,128)S(1)} %add.3), channel_id=1, replica_groups=mesh['layer'=4,'chip'=64,'core'=2] {'chip'}, dimensions={0} | all-to-all | bytes 1048576 | tf_op jit(solution)/shard_map/all_to_all | solution.py:229
  213.5 0.1 reduce_sum.9.own_ref
  213.6 0.0 copy-start.3
  213.7 23.1 %all_to_all.17.mine_ref = f32[64,16,128]{2,1,0:T(8,128)S(1)} all-to-all(f32[64,16,128]{2,1,0:T(8,128)S(1)} %broadcast_in_dim.4), channel_id=1, replica_groups=mesh['layer'=4,'chip'=64,'core'=2] {'chip'}, dimensions={0} | all-to-all | bytes 1048576 | tf_op jit(solution)/shard_map/all_to_all | solution.py:232
  236.7 0.0 copy-start
  236.8 5.8 %collective-permute-start.3 = (f32[64,16,128]{2,1,0:T(8,128)S(1)}, f32[64,16,128]{2,1,0:T(8,128)S(1)}, u32[]{:S(2)}, u32[]{:S(2)}) collective-permute-start(f32[64,16,128]{2,1,0:T(8,128)S(1)} %all_to_all.17.mine_ref), channel_id=1, source_target_pairs={{0,1},{1,0},{2,3},{3,2},{4,5},{5,4},{6,7},{7,6},{8,9},{9,8},{10,11... | collective-permute-start | bytes 1572872 | tf_op jit(solution)/shard_map/ppermute | solution.py:233
  242.6 1.5 collective-permute-done.3.other_ref
  244.1 0.0 copy-done.3
  244.1 0.0 copy-done
  244.1 0.0 copy-start.2
  244.1 0.8 copy-done.2
  244.9 6.9 %ortho.1 = (bf16[768,128]{1,0:T(8,128)(2,1)}, f32[16,128]{1,0:T(8,128)}) custom-call(s32[1]{0:T(128)} %bitcast.refs_0_.core_ref, f32[64,16,128]{2,1,0:T(8,128)} %copy-done, f32[64,16,128]{2,1,0:T(8,128)} %copy-done.2, f32[16,128]{1,0:T(8,128)} %copy-done.3, bf16[768,2048]{1,0:T(8,128)(2,1)} %bitcast.6), custom_call_target="tpu_custom_call" | custom-call | tf_op jit(solution)/shard_map/ortho/pallas_call | solution.py:192
  (2 shorter events, 0.0 us)
Async XLA Ops:
  0.6 17.3 %collective-permute-start.1 = (bf16[128,2048]{1,0:T(8,128)(2,1)}, bf16[128,2048]{1,0:T(8,128)(2,1)S(1)}, u32[]{:S(2)}, u32[]{:S(2)}) collective-permute-start(bf16[128,2048]{1,0:T(8,128)(2,1)} %refs_2_.1), channel_id=1, source_target_pairs={{0,1},{1,0},{2,3},{3,2},{4,5},{5,4},{6,7},{7,6},{8,9},{9,8},{10,11... | collective-permute-start | bytes 1572872 | tf_op jit(solution)/shard_map/ppermute | solution.py:220
  10.1 3.2 %copy-start.4 = (bf16[16,128]{1,0:T(8,128)(2,1)}, bf16[16,128]{1,0:T(8,128)(2,1)S(1)}, u32[]{:S(2)}) copy-start(bf16[16,128]{1,0:T(8,128)(2,1)S(1)} %convert_element_type.10.refs_3_) | copy-start | bytes 12292
  10.8 2.5 %copy-start.5 = (bf16[8,128]{1,0:T(8,128)(2,1)}, bf16[8,128]{1,0:T(8,128)(2,1)S(1)}, u32[]{:S(2)}) copy-start(bf16[8,128]{1,0:T(8,128)(2,1)S(1)} %convert_bitcast_fusion.refs_1_) | copy-start | bytes 6148
  10.8 5.9 %collective-permute-start = (bf16[24,128]{1,0:T(8,128)(2,1)S(1)}, bf16[24,128]{1,0:T(8,128)(2,1)S(1)}, u32[]{:S(2)}, u32[]{:S(2)}) collective-permute-start(bf16[24,128]{1,0:T(8,128)(2,1)S(1)} %pad_maximum_fusion), channel_id=1, source_target_pairs={{0,1},{1,0},{2,3},{3,2},{4,5},{5,4},{6,7},{7,6},{8,9},{9,8},{10,11... | collective-permute-start | bytes 18440 | tf_op jit(solution)/shard_map/ppermute | solution.py:221
  17.9 0.8 copy-start.1
  172.8 7.9 %collective-permute-start.2 = (f32[64,16,128]{2,1,0:T(8,128)}, f32[64,16,128]{2,1,0:T(8,128)S(1)}, u32[]{:S(2)}, u32[]{:S(2)}) collective-permute-start(f32[64,16,128]{2,1,0:T(8,128)} %get-tuple-element.7), channel_id=1, source_target_pairs={{0,1},{1,0},{2,3},{3,2},{4,5},{5,4},{6,7},{7,6},{8,9},{9,8},{10,11... | collective-permute-start | bytes 1572872 | tf_op jit(solution)/shard_map/ppermute | solution.py:228
  213.6 30.5 %copy-start.3 = (f32[16,128]{1,0:T(8,128)}, f32[16,128]{1,0:T(8,128)S(1)}, u32[]{:S(2)}) copy-start(f32[16,128]{1,0:T(8,128)S(1)} %reduce_sum.9.own_ref) | copy-start | bytes 24580
  236.7 7.3 %copy-start = (f32[64,16,128]{2,1,0:T(8,128)}, f32[64,16,128]{2,1,0:T(8,128)S(1)}, u32[]{:S(2)}) copy-start(f32[64,16,128]{2,1,0:T(8,128)S(1)} %all_to_all.17.mine_ref) | copy-start | bytes 1572868
  236.8 7.3 %collective-permute-start.3 = (f32[64,16,128]{2,1,0:T(8,128)S(1)}, f32[64,16,128]{2,1,0:T(8,128)S(1)}, u32[]{:S(2)}, u32[]{:S(2)}) collective-permute-start(f32[64,16,128]{2,1,0:T(8,128)S(1)} %all_to_all.17.mine_ref), channel_id=1, source_target_pairs={{0,1},{1,0},{2,3},{3,2},{4,5},{5,4},{6,7},{7,6},{8,9},{9,8},{10,11... | collective-permute-start | bytes 1572872 | tf_op jit(solution)/shard_map/ppermute | solution.py:233
  244.1 0.8 copy-start.2

commit v5 on v4

--- a/solution.py
+++ b/solution.py
@@ -31,14 +31,16 @@
     return jnp.where(flag, 1.0, 0.0).astype(BF)
 
 
-def pack_kernel(main_steps, spare, side_ref, ids_ref, rows_ref, basis_ref, *rest):
+def pack_kernel(main_steps, spare, mirrored, core_ref, small_ref, rows_ref, *rest):
     out_ref, buf, fan, sems = rest[-4:]
-    core, slot = side_ref[0], side_ref[1]
-    tops, row_count = ids_ref.shape
+    core = core_ref[0]
+    slot = 1 - core if mirrored else core
+    tops = small_ref.shape[0] - STEP
+    row_count = rows_ref.shape[0]
     chips = out_ref.shape[0]
     steps = main_steps + spare + 1
     copies = [pltpu.make_async_copy(buf.at[i], out_ref.at[:, 2 * i + slot], sems.at[i]) for i in range(steps)]
-    buf[steps - 1] = jnp.broadcast_to(basis_ref[...][None], (chips, STEP, LANES))
+    buf[steps - 1] = jnp.broadcast_to(small_ref[tops:, :].astype(BF)[None], (chips, STEP, LANES))
     copies[steps - 1].start()
     values = rows_ref[...].astype(F32)
     power = jnp.mean(values * values, axis=1, keepdims=True) + epsilon
@@ -46,7 +48,7 @@
     owner_names = (2 * iota((chips, row_count), 0) + core).astype(F32)
     member = jnp.zeros((chips, row_count), F32)
     for top in range(tops):
-        named = jnp.broadcast_to(ids_ref[top:top + 1, :].astype(F32), (chips, row_count))
+        named = jnp.broadcast_to(small_ref[top:top + 1, :], (chips, row_count))
         member = member + jnp.where(named == owner_names, 1.0, 0.0)
     ahead = as_bf16(iota((row_count, row_count), 0) <= iota((row_count, row_count), 1))
     rank = jnp.where(member > 0.0, dot(member.astype(BF), ahead), 0.0)
@@ -71,25 +73,25 @@
         copy.wait()
 
 
-def pack(side, ids, rows, basis, filled, chips, spare):
+def pack(core, small, rows, filled, chips, spare):
     main_steps = rows.shape[1] // (2 * LANES)
     steps = main_steps + spare + 1
     vmem = pl.BlockSpec(memory_space=pltpu.VMEM)
     hbm = pl.BlockSpec(memory_space=pl.ANY)
     return pl.pallas_call(
-        lambda *refs: pack_kernel(main_steps, spare, *refs),
+        lambda *refs: pack_kernel(main_steps, spare, bool(filled), *refs),
         out_shape=jax.ShapeDtypeStruct((chips, 2 * steps, STEP, LANES), BF),
-        in_specs=[pl.BlockSpec(memory_space=pltpu.SMEM), vmem, vmem, vmem] + [hbm] * len(filled),
+        in_specs=[pl.BlockSpec(memory_space=pltpu.SMEM), vmem, vmem] + [hbm] * len(filled),
         out_specs=hbm,
         scratch_shapes=[
             pltpu.VMEM((steps, chips, STEP, LANES), BF),
             pltpu.VMEM((spare, chips * STEP, LANES), F32),
             pltpu.SemaphoreType.DMA((steps,)),
         ],
-        input_output_aliases={4: 0} if filled else {},
+        input_output_aliases={3: 0} if filled else {},
         cost_estimate=pl.CostEstimate(flops=400_000_000, bytes_accessed=4_000_000, transcendentals=0),
         name="pack",
-    )(side, ids, rows, basis, *filled)
+    )(core, small, rows, *filled)
 
 
 def chain_kernel(main_steps, spare, core_ref, got_ref, weight_ref, keep_ref, send_ref, buf, x, w, fan, y, sems, w_sem):
@@ -215,14 +217,11 @@
     chips = experts // 2
     core = lax.axis_index("core").astype(jnp.int32).reshape(1)
     swap = [(0, 1), (1, 0)]
-    tops = expert_ids.shape[1]
-    small = jnp.concatenate([expert_ids.T.astype(BF), start_basis.astype(BF)], axis=0)
+    small = jnp.concatenate([expert_ids.T.astype(F32), start_basis], axis=0)
     rows_there = lax.ppermute(rows, "core", swap)
     small_there = lax.ppermute(small, "core", swap)
-    here = jnp.concatenate([core, core])
-    there = jnp.concatenate([core, 1 - core])
-    sent = pack(here, small[:tops], rows, small[tops:], (), chips, spare)
-    sent = pack(there, small_there[:tops], rows_there, small_there[tops:], (sent,), chips, spare)
+    sent = pack(core, small, rows, (), chips, spare)
+    sent = pack(core, small_there, rows_there, (sent,), chips, spare)
     got = lax.all_to_all(sent, "chip", split_axis=0, concat_axis=0, tiled=True)
     keep, send = chain(core, got, weight, spare)
     half = keep + lax.ppermute(send, "core", swap)

time: 252 us -> 252 us (level)
  no operation moved by 1% of the time
where the time goes in v5:
time: 252 us; the launch traced here: 251 us
  blocking collectives  194 us (77%)
  Pallas kernels  25 us (10%)
  starting transfers between devices  22.8 us (9%)
  waiting for transfers between devices  3.25 us (1%)
  other arithmetic  2.57 us (1%)
    all_to_all x1, blocking collectives, shards(): got = lax.all_to_all(sent, 'chip', split_axis=0, concat_axis=0, tiled=True)  139 us
    all_to_all x1, blocking collectives, shards(): lax.all_to_all(half, 'chip', split_axis=0, concat_axis=0, tiled=True)  31.9 us
    all_to_all x1, blocking collectives, shards(): lax.all_to_all(spread, 'chip', split_axis=0, concat_axis=0, tiled=True)  23.1 us
    pallas_call x1, Pallas kernels, chain(): pl.pallas_call(lambda *refs: chain_kernel(main_steps, spare, *refs), out_...  11.3 us
    ppermute x1, starting transfers between devices, shards(): rows_there = lax.ppermute(rows, 'core', swap)  8.75 us
    pallas_call x2, Pallas kernels, pack(): pl.pallas_call(lambda *refs: pack_kernel(main_steps, spare, bool(filled),...  6.86 us
    pallas_call x1, Pallas kernels, ortho(): pl.pallas_call(ortho_kernel, out_shape=(jax.ShapeDtypeStruct((weight.shap...  6.85 us
    ppermute x1, starting transfers between devices, shards(): half = keep + lax.ppermute(send, 'core', swap)  6.34 us
  transfers between devices with their start and end apart: 4, of which 2 were waited for; matrix products, arithmetic and copies ran while one was open for 1% of the time, Pallas kernels for 1%

profile of v5, /device:TPU:1, one launch (start us, length us, event | category | flops | bytes accessed | tf_op | source)
XLA Modules:
  0.0 251.1 jit_solution(7857194324139747404)
XLA Ops:
  0.6 8.7 %collective-permute-start.1 = (bf16[128,2048]{1,0:T(8,128)(2,1)}, bf16[128,2048]{1,0:T(8,128)(2,1)S(1)}, u32[]{:S(2)}, u32[]{:S(2)}) collective-permute-start(bf16[128,2048]{1,0:T(8,128)(2,1)} %refs_2_.1), channel_id=1, source_target_pairs={{0,1},{1,0},{2,3},{3,2},{4,5},{5,4},{6,7},{7,6},{8,9},{9,8},{10,11... | collective-permute-start | bytes 1572872 | tf_op jit(solution)/shard_map/ppermute | solution.py:221
  9.4 0.7 convert_bitcast_fusion
  10.1 0.7 pad_maximum_fusion.refs_1_
  10.8 0.0 copy-start.4
  10.8 1.9 collective-permute-start
  12.7 0.0 copy-done.4
  12.7 3.4 %pack.2.refs_3_ = bf16[64,22,16,128]{3,2,1,0:T(8,128)(2,1)} custom-call(s32[1]{0:T(128)} %bitcast.refs_0_.core_ref, f32[24,128]{1,0:T(8,128)} %copy-done.4, bf16[128,2048]{1,0:T(8,128)(2,1)} %refs_2_.1), custom_call_target="tpu_custom_call" | custom-call | flops 400000000 | bytes 4000000 | tf_op jit(solution)/shard_map/pack/pallas_call | solution.py:81
  16.1 0.0 collective-permute-done.refs_1_
  16.1 0.0 copy-start.5
  16.1 0.0 collective-permute-done.1.refs_2_
  16.1 0.6 copy-done.5
  16.7 0.0 copy-start.1
  16.7 0.8 copy-done.1
  17.5 3.5 %pack.3 = bf16[64,22,16,128]{3,2,1,0:T(8,128)(2,1)} custom-call(s32[1]{0:T(128)} %bitcast.refs_0_.core_ref, f32[24,128]{1,0:T(8,128)} %copy-done.5, bf16[128,2048]{1,0:T(8,128)(2,1)} %copy-done.1, bf16[64,22,16,128]{3,2,1,0:T(8,128)(2,1)} %pack.2.refs_3_), custom_call_target="tpu_custom_call", output_to_operand_aliasing={{}: (3, {})} | custom-call | flops 400000000 | bytes 4000000 | tf_op jit(solution)/shard_map/pack/pallas_call | solution.py:81
  21.0 139.4 %all_to_all.15.refs_1_ = bf16[64,22,16,128]{3,2,1,0:T(8,128)(2,1)} all-to-all(bf16[64,22,16,128]{3,2,1,0:T(8,128)(2,1)} %pack.3), channel_id=1, replica_groups=mesh['layer'=4,'chip'=64,'core'=2] {'chip'}, dimensions={0} | all-to-all | bytes 11534336 | tf_op jit(solution)/shard_map/all_to_all | solution.py:225
  160.4 11.3 %chain.1 = (f32[64,16,128]{2,1,0:T(8,128)}, f32[64,16,128]{2,1,0:T(8,128)}) custom-call(s32[1]{0:T(128)} %bitcast.refs_0_.core_ref, bf16[64,22,16,128]{3,2,1,0:T(8,128)(2,1)} %all_to_all.15.refs_1_, bf16[768,2048]{1,0:T(8,128)(2,1)} %bitcast.5), custom_call_target="tpu_custom_call" | custom-call | tf_op jit(solution)/shard_map/chain/pallas_call | solution.py:147
  171.7 6.3 %collective-permute-start.2 = (f32[64,16,128]{2,1,0:T(8,128)}, f32[64,16,128]{2,1,0:T(8,128)S(1)}, u32[]{:S(2)}, u32[]{:S(2)}) collective-permute-start(f32[64,16,128]{2,1,0:T(8,128)} %get-tuple-element.7), channel_id=1, source_target_pairs={{0,1},{1,0},{2,3},{3,2},{4,5},{5,4},{6,7},{7,6},{8,9},{9,8},{10,11... | collective-permute-start | bytes 1572872 | tf_op jit(solution)/shard_map/ppermute | solution.py:227
  178.0 1.7 collective-permute-done.2
  179.7 1.1 add.3
  180.9 31.9 %all_to_all.16 = f32[64,16,128]{2,1,0:T(8,128)S(1)} all-to-all(f32[64,16,128]{2,1,0:T(8,128)S(1)} %add.3), channel_id=1, replica_groups=mesh['layer'=4,'chip'=64,'core'=2] {'chip'}, dimensions={0} | all-to-all | bytes 1048576 | tf_op jit(solution)/shard_map/all_to_all | solution.py:228
  212.7 0.1 reduce_sum.9.own_ref
  212.8 0.0 copy-start.3
  212.8 23.1 %all_to_all.17.mine_ref = f32[64,16,128]{2,1,0:T(8,128)S(1)} all-to-all(f32[64,16,128]{2,1,0:T(8,128)S(1)} %broadcast_in_dim.4), channel_id=1, replica_groups=mesh['layer'=4,'chip'=64,'core'=2] {'chip'}, dimensions={0} | all-to-all | bytes 1048576 | tf_op jit(solution)/shard_map/all_to_all | solution.py:231
  235.9 0.0 copy-start
  235.9 5.8 %collective-permute-start.3 = (f32[64,16,128]{2,1,0:T(8,128)S(1)}, f32[64,16,128]{2,1,0:T(8,128)S(1)}, u32[]{:S(2)}, u32[]{:S(2)}) collective-permute-start(f32[64,16,128]{2,1,0:T(8,128)S(1)} %all_to_all.17.mine_ref), channel_id=1, source_target_pairs={{0,1},{1,0},{2,3},{3,2},{4,5},{5,4},{6,7},{7,6},{8,9},{9,8},{10,11... | collective-permute-start | bytes 1572872 | tf_op jit(solution)/shard_map/ppermute | solution.py:232
  241.7 1.5 collective-permute-done.3.other_ref
  243.3 0.0 copy-done.3
  243.3 0.0 copy-done
  243.3 0.0 copy-start.2
  243.3 0.8 copy-done.2
  244.0 6.9 %ortho.1 = (bf16[768,128]{1,0:T(8,128)(2,1)}, f32[16,128]{1,0:T(8,128)}) custom-call(s32[1]{0:T(128)} %bitcast.refs_0_.core_ref, f32[64,16,128]{2,1,0:T(8,128)} %copy-done, f32[64,16,128]{2,1,0:T(8,128)} %copy-done.2, f32[16,128]{1,0:T(8,128)} %copy-done.3, bf16[768,2048]{1,0:T(8,128)(2,1)} %bitcast.6), custom_call_target="tpu_custom_call" | custom-call | tf_op jit(solution)/shard_map/ortho/pallas_call | solution.py:194
  (1 shorter events, 0.0 us)
Async XLA Ops:
  0.6 15.5 %collective-permute-start.1 = (bf16[128,2048]{1,0:T(8,128)(2,1)}, bf16[128,2048]{1,0:T(8,128)(2,1)S(1)}, u32[]{:S(2)}, u32[]{:S(2)}) collective-permute-start(bf16[128,2048]{1,0:T(8,128)(2,1)} %refs_2_.1), channel_id=1, source_target_pairs={{0,1},{1,0},{2,3},{3,2},{4,5},{5,4},{6,7},{7,6},{8,9},{9,8},{10,11... | collective-permute-start | bytes 1572872 | tf_op jit(solution)/shard_map/ppermute | solution.py:221
  10.8 1.9 copy-start.4
  10.8 5.3 %collective-permute-start = (f32[24,128]{1,0:T(8,128)S(1)}, f32[24,128]{1,0:T(8,128)S(1)}, u32[]{:S(2)}, u32[]{:S(2)}) collective-permute-start(f32[24,128]{1,0:T(8,128)S(1)} %pad_maximum_fusion.refs_1_), channel_id=1, source_target_pairs={{0,1},{1,0},{2,3},{3,2},{4,5},{5,4},{6,7},{7,6},{8,9},{9,8},{10,11... | collective-permute-start | bytes 36872 | tf_op jit(solution)/shard_map/ppermute | solution.py:222
  16.1 0.6 copy-start.5
  16.7 0.8 copy-start.1
  171.7 8.1 %collective-permute-start.2 = (f32[64,16,128]{2,1,0:T(8,128)}, f32[64,16,128]{2,1,0:T(8,128)S(1)}, u32[]{:S(2)}, u32[]{:S(2)}) collective-permute-start(f32[64,16,128]{2,1,0:T(8,128)} %get-tuple-element.7), channel_id=1, source_target_pairs={{0,1},{1,0},{2,3},{3,2},{4,5},{5,4},{6,7},{7,6},{8,9},{9,8},{10,11... | collective-permute-start | bytes 1572872 | tf_op jit(solution)/shard_map/ppermute | solution.py:227
  212.8 30.5 %copy-start.3 = (f32[16,128]{1,0:T(8,128)}, f32[16,128]{1,0:T(8,128)S(1)}, u32[]{:S(2)}) copy-start(f32[16,128]{1,0:T(8,128)S(1)} %reduce_sum.9.own_ref) | copy-start | bytes 24580
  235.9 7.3 %copy-start = (f32[64,16,128]{2,1,0:T(8,128)}, f32[64,16,128]{2,1,0:T(8,128)S(1)}, u32[]{:S(2)}) copy-start(f32[64,16,128]{2,1,0:T(8,128)S(1)} %all_to_all.17.mine_ref) | copy-start | bytes 1572868
  235.9 7.3 %collective-permute-start.3 = (f32[64,16,128]{2,1,0:T(8,128)S(1)}, f32[64,16,128]{2,1,0:T(8,128)S(1)}, u32[]{:S(2)}, u32[]{:S(2)}) collective-permute-start(f32[64,16,128]{2,1,0:T(8,128)S(1)} %all_to_all.17.mine_ref), channel_id=1, source_target_pairs={{0,1},{1,0},{2,3},{3,2},{4,5},{5,4},{6,7},{7,6},{8,9},{9,8},{10,11... | collective-permute-start | bytes 1572872 | tf_op jit(solution)/shard_map/ppermute | solution.py:232
  243.3 0.8 copy-start.2
